TPU v7x, 32 devices: a whole 2x2x4 slice. The times are simulated.
32 devices in a mesh: grp: 2 (over x), ctx: 16 (over z, y, core).
Axes of the slice: x: 2, y: 2, z: 4, core: 2. Of those that a mesh axis runs over, the one named last changes fastest.
Arguments:
- queries: bfloat16 [16384, 2048], P(('grp', 'ctx')), parts along dimension 0, may hold values from -7 to 7
- keys: bfloat16 [16384, 512], P(('grp', 'ctx')), parts along dimension 0, may hold values from -6 to 6
- values: bfloat16 [16384, 512], P(('grp', 'ctx')), parts along dimension 0, may hold values from -6 to 6
- out_grad: bfloat16 [16384, 2048], P(('grp', 'ctx')), parts along dimension 0, may hold values from -6 to 6
- doc_starts: int32 [16], P('grp'), parts along dimension 0, may hold values from 0 to 7423, as said below
- block_lists: int32 [128, 6], P(('grp', 'ctx')), parts along dimension 0, may hold values from -1 to 63, as said below
Outputs:
- attended: bfloat16 [16384, 2048], P(('grp', 'ctx')), parts along dimension 0
- grad_queries: bfloat16 [16384, 2048], P(('grp', 'ctx')), parts along dimension 0
- grad_keys: bfloat16 [16384, 512], P(('grp', 'ctx')), parts along dimension 0
- grad_values: bfloat16 [16384, 512], P(('grp', 'ctx')), parts along dimension 0
There are 2 independent parts, one for each index of `grp`. A program takes and returns all parts, laid end to end along the dimension named above; each array names one. Nothing has to cross between parts.
Inputs may be any that keep to these rules, and one draw needn't show every extreme that they name: `block_lists`: row b lists block b first, then further distinct blocks before b that lie in the document of b's last token and among the blocks of b's device or of the 2 devices before it, then -1 in every slot left empty; the last row is full. `doc_starts`: Increasing, the first entry 0.
All inputs are finite; a program needn't handle non-finite values.
Results may differ from a plain program's by a relative error of at most 0.029.
Values may be sent and summed in bfloat16 or wider, within the bound.
No kernel may reach another device: no remote copies, remote signals or barrier semaphores. Data moves between devices by JAX's collectives and lax.ppermute only.
A program may use at most 128 MiB of HBM per device.

v0:
```python
import jax
import jax.numpy as jnp
from jax import lax
from jax.sharding import PartitionSpec as P

HD = 128
HEADS = 16
KV_HEADS = 4
BLOCK = 128
R_DEV = 2


def shifted(value, axis, steps):
    count = lax.axis_size(axis)
    initial, last = (max(0, -steps), min(count, count - steps))
    return lax.ppermute(value, axis, [(source, source + steps) for source in range(initial, last)])


def doc_index(positions, doc_starts):
    return jnp.sum((positions[..., None] >= doc_starts[1:]).astype(jnp.int32), axis=-1)


def allowed_mask(entries, block_index, doc_starts):
    offsets = jnp.arange(BLOCK, dtype=jnp.int32)
    listed = entries >= 0
    clamped = jnp.where(listed, entries, 0)
    query_pos = block_index * BLOCK + offsets
    key_pos = clamped[:, None] * BLOCK + offsets[None, :]
    same_doc = (
        doc_index(key_pos, doc_starts)[None] == doc_index(query_pos, doc_starts)[:, None, None]
    )
    causal = key_pos[None] <= query_pos[:, None, None]
    allowed = listed[None, :, None] & causal & same_doc
    return allowed.reshape(BLOCK, -1)


def softmax_rows(scores, allowed):
    masked = jnp.where(allowed, scores, -1e30)
    row_max = jnp.max(masked, axis=-1, keepdims=True)
    unnormed = jnp.where(allowed, jnp.exp(masked - row_max), 0.0)
    return unnormed / jnp.sum(unnormed, axis=-1, keepdims=True)


def attend_dense(query_blk, grad_blk, key_tiles, value_tiles, allowed, scaling):
    kv_heads, rows_all, width = query_blk.shape
    span = key_tiles.shape[1]
    scores = (
        jnp.einsum("hqd,hkd->hqk", query_blk, key_tiles, preferred_element_type=jnp.float32)
        * scaling
    )
    scores = scores.reshape(kv_heads, rows_all // BLOCK, BLOCK, span)
    attn_probs = softmax_rows(scores, allowed).reshape(kv_heads, rows_all, span)
    probs_low = attn_probs.astype(jnp.bfloat16)
    attended = jnp.einsum(
        "hqk,hkd->hqd", probs_low, value_tiles, preferred_element_type=jnp.float32
    ).astype(jnp.bfloat16)
    row_delta = jnp.einsum("hqd,hqd->hq", grad_blk, attended, preferred_element_type=jnp.float32)
    dprobs = jnp.einsum("hqd,hkd->hqk", grad_blk, value_tiles, preferred_element_type=jnp.float32)
    grad_scores = (attn_probs * (dprobs - row_delta[..., None])).astype(jnp.bfloat16)
    grad_query = (
        jnp.einsum("hqk,hkd->hqd", grad_scores, key_tiles, preferred_element_type=jnp.float32)
        * scaling
    ).astype(jnp.bfloat16)
    grad_key_tiles = (
        jnp.einsum("hqk,hqd->hkd", grad_scores, query_blk, preferred_element_type=jnp.float32)
        * scaling
    )
    grad_value_tiles = jnp.einsum(
        "hqk,hqd->hkd", probs_low, grad_blk, preferred_element_type=jnp.float32
    )
    return (attended, grad_query, grad_key_tiles, grad_value_tiles)


def heads_first(array, heads):
    return jnp.transpose(array.reshape(array.shape[0], heads, HD), (1, 0, 2))


def per_device(queries, keys, values, out_grad, doc_starts, block_lists):
    device = lax.axis_index("ctx")
    blocks = block_lists.shape[0]
    rows_dev = queries.shape[0]
    list_slots = block_lists.shape[1]
    groups = HEADS // KV_HEADS
    scaling = HD ** (-0.5)
    fetched = []
    for distance in range(1, R_DEV + 1):
        fetched.append(shifted((keys, values), "ctx", distance))
    ordered = fetched[::-1] + [(keys, values)]
    key_window = heads_first(
        jnp.concatenate([pair_item[0] for pair_item in ordered], axis=0), KV_HEADS
    )
    value_window = heads_first(
        jnp.concatenate([pair_item[1] for pair_item in ordered], axis=0), KV_HEADS
    )
    window_base = (device - R_DEV) * blocks
    first_block = device * blocks

    def to_blocks(array):
        shaped = array.reshape(blocks, BLOCK, KV_HEADS, groups, HD)
        return jnp.transpose(shaped, (0, 2, 3, 1, 4)).reshape(blocks, KV_HEADS, groups * BLOCK, HD)

    def from_blocks(array):
        shaped = array.reshape(blocks, KV_HEADS, groups, BLOCK, HD)
        return jnp.transpose(shaped, (0, 3, 1, 2, 4)).reshape(rows_dev, HEADS * HD)

    query_blocks = to_blocks(queries)
    grad_blocks = to_blocks(out_grad)

    def per_block(carried, inputs):
        acc_keys, acc_values = carried
        query_blk, grad_blk, entries, block_index = inputs
        listed = entries >= 0
        window_index = jnp.where(listed, entries - window_base, 0)
        key_tiles = jnp.concatenate(
            [
                lax.dynamic_slice_in_dim(key_window, window_index[slot] * BLOCK, BLOCK, 1)
                for slot in range(list_slots)
            ],
            axis=1,
        )
        value_tiles = jnp.concatenate(
            [
                lax.dynamic_slice_in_dim(value_window, window_index[slot] * BLOCK, BLOCK, 1)
                for slot in range(list_slots)
            ],
            axis=1,
        )
        allowed = allowed_mask(entries, block_index, doc_starts)
        attended, grad_query, grad_key_tiles, grad_value_tiles = attend_dense(
            query_blk, grad_blk, key_tiles, value_tiles, allowed, scaling
        )
        for slot in range(list_slots):
            start = window_index[slot] * BLOCK
            old_keys = lax.dynamic_slice_in_dim(acc_keys, start, BLOCK, 1)
            old_values = lax.dynamic_slice_in_dim(acc_values, start, BLOCK, 1)
            acc_keys = lax.dynamic_update_slice_in_dim(
                acc_keys, old_keys + grad_key_tiles[:, slot * BLOCK : (slot + 1) * BLOCK], start, 1
            )
            acc_values = lax.dynamic_update_slice_in_dim(
                acc_values,
                old_values + grad_value_tiles[:, slot * BLOCK : (slot + 1) * BLOCK],
                start,
                1,
            )
        return ((acc_keys, acc_values), (attended, grad_query))

    window_rows = (R_DEV + 1) * rows_dev
    zeros_acc = jnp.zeros((KV_HEADS, window_rows, HD), jnp.float32)
    indices = first_block + jnp.arange(blocks, dtype=jnp.int32)
    (acc_keys, acc_values), (attended, grad_query) = lax.scan(
        per_block, (zeros_acc, zeros_acc), (query_blocks, grad_blocks, block_lists, indices)
    )
    slab_keys = jnp.transpose(acc_keys, (1, 0, 2)).reshape(R_DEV + 1, rows_dev, KV_HEADS * HD)
    slab_values = jnp.transpose(acc_values, (1, 0, 2)).reshape(R_DEV + 1, rows_dev, KV_HEADS * HD)
    summed_keys = slab_keys[R_DEV]
    summed_values = slab_values[R_DEV]
    for distance in range(1, R_DEV + 1):
        returned = shifted(
            (slab_keys[R_DEV - distance], slab_values[R_DEV - distance]), "ctx", -distance
        )
        summed_keys = summed_keys + returned[0]
        summed_values = summed_values + returned[1]
    return (
        from_blocks(attended),
        from_blocks(grad_query),
        summed_keys.astype(jnp.bfloat16),
        summed_values.astype(jnp.bfloat16),
    )


def solution(mesh):
    placed = (
        P(("grp", "ctx"), None),
        P(("grp", "ctx"), None),
        P(("grp", "ctx"), None),
        P(("grp", "ctx"), None),
        P("grp"),
        P(("grp", "ctx"), None),
    )
    return jax.shard_map(
        per_device,
        mesh=mesh,
        in_specs=placed,
        out_specs=(
            P(("grp", "ctx"), None),
            P(("grp", "ctx"), None),
            P(("grp", "ctx"), None),
            P(("grp", "ctx"), None),
        ),
        check_vma=False,
    )
```

profile of v0, /device:TPU:22, one launch (start us, length us, event | category | flops | bytes accessed | tf_op | source)
XLA Modules:
  0.0 329.9 jit_solution(5780523535233906854)
XLA Ops:
  3.8 3.4 %collective-permute-start.2 = (bf16[512,512]{0,1:T(8,128)(2,1)S(1)}, bf16[512,512]{0,1:T(8,128)(2,1)}, u32[]{:S(2)}, u32[]{:S(2)}) collective-permute-start(bf16[512,512]{0,1:T(8,128)(2,1)S(1)} %copy.49), channel_id=1, source_target_pairs={{0,2},{1,3},{2,4},{3,5},{4,6},{5,7},{6,8},{7,9},{8,10},{9,11},{10,... | collective-permute-start | bytes 1572872 | tf_op jit(solution)/shard_map/ppermute | solution.py:16
  8.5 3.3 collective-permute-start.1
  14.0 3.2 reshape.158
  19.1 3.2 reshape.161
  27.3 7.7 %collective-permute-done.1 = bf16[512,512]{0,1:T(8,128)(2,1)} collective-permute-done((bf16[512,512]{0,1:T(8,128)(2,1)S(1)}, bf16[512,512]{0,1:T(8,128)(2,1)}, u32[]{:S(2)}, u32[]{:S(2)}) %collective-permute-start.1) | collective-permute-done | bytes 524320 | tf_op jit(solution)/shard_map/ppermute | solution.py:16
  40.0 202.9 %while.16 = (s32[]{:T(128)}, f32[4,1536,128]{2,1,0:T(8,128)}, f32[4,1536,128]{2,1,0:T(8,128)S(1)}, bf16[4,4,512,128]{3,2,1,0:T(8,128)(2,1)}, bf16[4,4,512,128]{3...) while((s32[]{:T(128)}, f32[4,1536,128]{2,1,0:T(8,128)}, ...), condition=%wide.region_5.6_spmd, body=%wide.region_0.5_spmd.sunk | while | flops 2436646912 | bytes 115217560 | solution.py:150
  65.7 6.8 %fusion.113 = (f32[4,512]{1,0:T(4,128)S(1)}, f32[4,512,768]{2,1,0:T(8,128)}) fusion(pred[512,768]{1,0:T(8,128)(4,1)S(1)} %bitcast.181, bf16[4,768,128]{2,1,0:T(8,128)(2,1)} %dynamic-slice_dynamic-update-slice_fusion.29, bf16[4,4,512,128]{3,2,1,0:T(8,128)(2,1)} %get-tuple-element.300, s32[]{:T(128)S(6)} %copy.118), kind=kOutput, calls=%fused_computation.110.clone.1 | convolution fusion | flops 410518272 | bytes 8396804 | tf_op jit(solution)/shard_map/while/body/eval_jaxpr/sub | solution.py:40
  72.5 3.4 %fusion.114 = bf16[4,512,768]{2,1,0:T(8,128)(2,1)S(1)} fusion(f32[4,512,768]{2,1,0:T(8,128)} %get-tuple-element.251, f32[4,512]{1,0:T(4,128)S(1)} %get-tuple-element.252), kind=kLoop, calls=%fused_computation.9.clone.1 | loop fusion | flops 3145728 | bytes 9445376 | tf_op jit(solution)/shard_map/while/body/eval_jaxpr/convert_element_type | solution.py:53
  75.9 2.5 fusion.116
  82.1 2.9 fusion.128
  116.4 6.8 %fusion.113 = (f32[4,512]{1,0:T(4,128)S(1)}, f32[4,512,768]{2,1,0:T(8,128)}) fusion(pred[512,768]{1,0:T(8,128)(4,1)S(1)} %bitcast.181, bf16[4,768,128]{2,1,0:T(8,128)(2,1)} %dynamic-slice_dynamic-update-slice_fusion.29, bf16[4,4,512,128]{3,2,1,0:T(8,128)(2,1)} %get-tuple-element.300, s32[]{:T(128)S(6)} %copy.118), kind=kOutput, calls=%fused_computation.110.clone.1 | convolution fusion | flops 410518272 | bytes 8396804 | tf_op jit(solution)/shard_map/while/body/eval_jaxpr/sub | solution.py:40
  123.2 3.4 %fusion.114 = bf16[4,512,768]{2,1,0:T(8,128)(2,1)S(1)} fusion(f32[4,512,768]{2,1,0:T(8,128)} %get-tuple-element.251, f32[4,512]{1,0:T(4,128)S(1)} %get-tuple-element.252), kind=kLoop, calls=%fused_computation.9.clone.1 | loop fusion | flops 3145728 | bytes 9445376 | tf_op jit(solution)/shard_map/while/body/eval_jaxpr/convert_element_type | solution.py:53
  126.6 2.5 fusion.116
  132.8 2.9 fusion.128
  167.1 6.8 %fusion.113 = (f32[4,512]{1,0:T(4,128)S(1)}, f32[4,512,768]{2,1,0:T(8,128)}) fusion(pred[512,768]{1,0:T(8,128)(4,1)S(1)} %bitcast.181, bf16[4,768,128]{2,1,0:T(8,128)(2,1)} %dynamic-slice_dynamic-update-slice_fusion.29, bf16[4,4,512,128]{3,2,1,0:T(8,128)(2,1)} %get-tuple-element.300, s32[]{:T(128)S(6)} %copy.118), kind=kOutput, calls=%fused_computation.110.clone.1 | convolution fusion | flops 410518272 | bytes 8396804 | tf_op jit(solution)/shard_map/while/body/eval_jaxpr/sub | solution.py:40
  173.9 3.4 %fusion.114 = bf16[4,512,768]{2,1,0:T(8,128)(2,1)S(1)} fusion(f32[4,512,768]{2,1,0:T(8,128)} %get-tuple-element.251, f32[4,512]{1,0:T(4,128)S(1)} %get-tuple-element.252), kind=kLoop, calls=%fused_computation.9.clone.1 | loop fusion | flops 3145728 | bytes 9445376 | tf_op jit(solution)/shard_map/while/body/eval_jaxpr/convert_element_type | solution.py:53
  177.3 2.5 fusion.116
  183.5 2.9 fusion.128
  217.8 6.8 %fusion.113 = (f32[4,512]{1,0:T(4,128)S(1)}, f32[4,512,768]{2,1,0:T(8,128)}) fusion(pred[512,768]{1,0:T(8,128)(4,1)S(1)} %bitcast.181, bf16[4,768,128]{2,1,0:T(8,128)(2,1)} %dynamic-slice_dynamic-update-slice_fusion.29, bf16[4,4,512,128]{3,2,1,0:T(8,128)(2,1)} %get-tuple-element.300, s32[]{:T(128)S(6)} %copy.118), kind=kOutput, calls=%fused_computation.110.clone.1 | convolution fusion | flops 410518272 | bytes 8396804 | tf_op jit(solution)/shard_map/while/body/eval_jaxpr/sub | solution.py:40
  224.6 3.4 %fusion.114 = bf16[4,512,768]{2,1,0:T(8,128)(2,1)S(1)} fusion(f32[4,512,768]{2,1,0:T(8,128)} %get-tuple-element.251, f32[4,512]{1,0:T(4,128)S(1)} %get-tuple-element.252), kind=kLoop, calls=%fused_computation.9.clone.1 | loop fusion | flops 3145728 | bytes 9445376 | tf_op jit(solution)/shard_map/while/body/eval_jaxpr/convert_element_type | solution.py:53
  234.3 2.9 fusion.128
  242.9 3.0 slice_bitcast_fusion.5
  248.2 8.3 %collective-permute-start.4 = (f32[512,512]{1,0:T(8,128)}, f32[512,512]{1,0:T(8,128)}, u32[]{:S(2)}, u32[]{:S(2)}) collective-permute-start(f32[512,512]{1,0:T(8,128)} %bitcast.116), channel_id=1, source_target_pairs={{1,0},{2,1},{3,2},{4,3},{5,4},{6,5},{7,6},{8,7},{9,8},{10,9},{11,1... | collective-permute-start | bytes 3145736 | tf_op jit(solution)/shard_map/ppermute | solution.py:16
  264.4 3.5 %collective-permute-start.7 = (f32[512,512]{1,0:T(8,128)}, f32[512,512]{1,0:T(8,128)}, u32[]{:S(2)}, u32[]{:S(2)}) collective-permute-start(f32[512,512]{1,0:T(8,128)} %bitcast.113), channel_id=1, source_target_pairs={{2,0},{3,1},{4,2},{5,3},{6,4},{7,5},{8,6},{9,7},{10,8},{11,9},{12,... | collective-permute-start | bytes 3145736 | tf_op jit(solution)/shard_map/ppermute | solution.py:16
  269.6 2.8 reshape.167
  272.4 3.2 copy.84
  275.6 2.8 reshape.165
  279.0 24.4 %collective-permute-done.5 = f32[512,512]{1,0:T(8,128)} collective-permute-done((f32[512,512]{1,0:T(8,128)}, f32[512,512]{1,0:T(8,128)}, u32[]{:S(2)}, u32[]{:S(2)}) %collective-permute-start.5) | collective-permute-done | bytes 1048608 | tf_op jit(solution)/shard_map/ppermute | solution.py:16
  303.5 2.6 fusion.55
  306.0 8.1 %collective-permute-done.6 = f32[512,512]{1,0:T(8,128)} collective-permute-done((f32[512,512]{1,0:T(8,128)}, f32[512,512]{1,0:T(8,128)}, u32[]{:S(2)}, u32[]{:S(2)}) %collective-permute-start.6) | collective-permute-done | bytes 1048608 | tf_op jit(solution)/shard_map/ppermute | solution.py:16
  314.1 13.2 %collective-permute-done.7 = f32[512,512]{1,0:T(8,128)} collective-permute-done((f32[512,512]{1,0:T(8,128)}, f32[512,512]{1,0:T(8,128)}, u32[]{:S(2)}, u32[]{:S(2)}) %collective-permute-start.7) | collective-permute-done | bytes 1048608 | tf_op jit(solution)/shard_map/ppermute | solution.py:16
  327.4 2.6 fusion.53
  (262 shorter events, 155.4 us)
Async XLA Ops:
  1.9 22.5 %collective-permute-start.3 = (bf16[512,512]{0,1:T(8,128)(2,1)S(1)}, bf16[512,512]{0,1:T(8,128)(2,1)}, u32[]{:S(2)}, u32[]{:S(2)}) collective-permute-start(bf16[512,512]{0,1:T(8,128)(2,1)S(1)} %copy.49), channel_id=1, source_target_pairs={{0,1},{1,2},{2,3},{3,4},{4,5},{5,6},{6,7},{7,8},{8,9},{9,10},{10,1... | collective-permute-start | bytes 1572872 | tf_op jit(solution)/shard_map/ppermute | solution.py:16
  3.8 20.6 %collective-permute-start.2 = (bf16[512,512]{0,1:T(8,128)(2,1)S(1)}, bf16[512,512]{0,1:T(8,128)(2,1)}, u32[]{:S(2)}, u32[]{:S(2)}) collective-permute-start(bf16[512,512]{0,1:T(8,128)(2,1)S(1)} %copy.49), channel_id=1, source_target_pairs={{0,2},{1,3},{2,4},{3,5},{4,6},{5,7},{6,8},{7,9},{8,10},{9,11},{10,... | collective-permute-start | bytes 1572872 | tf_op jit(solution)/shard_map/ppermute | solution.py:16
  8.5 26.5 %collective-permute-start.1 = (bf16[512,512]{0,1:T(8,128)(2,1)S(1)}, bf16[512,512]{0,1:T(8,128)(2,1)}, u32[]{:S(2)}, u32[]{:S(2)}) collective-permute-start(bf16[512,512]{0,1:T(8,128)(2,1)S(1)} %copy.45), channel_id=1, source_target_pairs={{0,1},{1,2},{2,3},{3,4},{4,5},{5,6},{6,7},{7,8},{8,9},{9,10},{10,1... | collective-permute-start | bytes 1572872 | tf_op jit(solution)/shard_map/ppermute | solution.py:16
  11.8 23.2 %collective-permute-start = (bf16[512,512]{0,1:T(8,128)(2,1)S(1)}, bf16[512,512]{0,1:T(8,128)(2,1)}, u32[]{:S(2)}, u32[]{:S(2)}) collective-permute-start(bf16[512,512]{0,1:T(8,128)(2,1)S(1)} %copy.45), channel_id=1, source_target_pairs={{0,2},{1,3},{2,4},{3,5},{4,6},{5,7},{6,8},{7,9},{8,10},{9,11},{10,... | collective-permute-start | bytes 1572872 | tf_op jit(solution)/shard_map/ppermute | solution.py:16
  37.9 2.1 copy-start.7
  72.5 3.4 %copy-start.2 = (bf16[4,4,512,128]{3,2,1,0:T(8,128)(2,1)S(1)}, bf16[4,4,512,128]{3,2,1,0:T(8,128)(2,1)}, u32[]{:S(2)}) copy-start(bf16[4,4,512,128]{3,2,1,0:T(8,128)(2,1)} %get-tuple-element.302) | copy-start | bytes 6291460 | tf_op jit(solution)/shard_map/while
  72.5 7.2 %slice-start = ((s8[6291456]{0:T(1024)(128)(4,1)}), s8[4194304]{0:T(1024)(128)(4,1)S(1)}, s32[]{:S(2)}) async-start(s8[6291456]{0:T(1024)(128)(4,1)} %bitcast.175), calls=%async_computation | async-start | bytes 8388608 | tf_op jit(solution)/shard_map/while
  75.9 3.8 %slice-start.1 = ((s8[6291456]{0:T(1024)(128)(4,1)}), s8[2097152]{0:T(1024)(128)(4,1)S(1)}, s32[]{:S(2)}) async-start(s8[6291456]{0:T(1024)(128)(4,1)} %bitcast.175), calls=%async_computation.1 | async-start | bytes 4194304 | tf_op jit(solution)/shard_map/while
  85.0 3.3 %copy-start = (f32[4,1536,128]{2,1,0:T(8,128)S(1)}, f32[4,1536,128]{2,1,0:T(8,128)}, u32[]{:S(2)}) copy-start(f32[4,1536,128]{2,1,0:T(8,128)} %get-tuple-element.275) | copy-start | bytes 9437188 | tf_op jit(solution)/shard_map/while
  88.5 2.2 copy-start.9
  123.2 3.4 %copy-start.2 = (bf16[4,4,512,128]{3,2,1,0:T(8,128)(2,1)S(1)}, bf16[4,4,512,128]{3,2,1,0:T(8,128)(2,1)}, u32[]{:S(2)}) copy-start(bf16[4,4,512,128]{3,2,1,0:T(8,128)(2,1)} %get-tuple-element.302) | copy-start | bytes 6291460 | tf_op jit(solution)/shard_map/while
  123.2 7.2 %slice-start = ((s8[6291456]{0:T(1024)(128)(4,1)}), s8[4194304]{0:T(1024)(128)(4,1)S(1)}, s32[]{:S(2)}) async-start(s8[6291456]{0:T(1024)(128)(4,1)} %bitcast.175), calls=%async_computation | async-start | bytes 8388608 | tf_op jit(solution)/shard_map/while
  126.6 3.8 %slice-start.1 = ((s8[6291456]{0:T(1024)(128)(4,1)}), s8[2097152]{0:T(1024)(128)(4,1)S(1)}, s32[]{:S(2)}) async-start(s8[6291456]{0:T(1024)(128)(4,1)} %bitcast.175), calls=%async_computation.1 | async-start | bytes 4194304 | tf_op jit(solution)/shard_map/while
  135.8 3.3 %copy-start = (f32[4,1536,128]{2,1,0:T(8,128)S(1)}, f32[4,1536,128]{2,1,0:T(8,128)}, u32[]{:S(2)}) copy-start(f32[4,1536,128]{2,1,0:T(8,128)} %get-tuple-element.275) | copy-start | bytes 9437188 | tf_op jit(solution)/shard_map/while
  139.3 2.2 copy-start.9
  173.9 3.4 %copy-start.2 = (bf16[4,4,512,128]{3,2,1,0:T(8,128)(2,1)S(1)}, bf16[4,4,512,128]{3,2,1,0:T(8,128)(2,1)}, u32[]{:S(2)}) copy-start(bf16[4,4,512,128]{3,2,1,0:T(8,128)(2,1)} %get-tuple-element.302) | copy-start | bytes 6291460 | tf_op jit(solution)/shard_map/while
  173.9 7.2 %slice-start = ((s8[6291456]{0:T(1024)(128)(4,1)}), s8[4194304]{0:T(1024)(128)(4,1)S(1)}, s32[]{:S(2)}) async-start(s8[6291456]{0:T(1024)(128)(4,1)} %bitcast.175), calls=%async_computation | async-start | bytes 8388608 | tf_op jit(solution)/shard_map/while
  177.3 3.8 %slice-start.1 = ((s8[6291456]{0:T(1024)(128)(4,1)}), s8[2097152]{0:T(1024)(128)(4,1)S(1)}, s32[]{:S(2)}) async-start(s8[6291456]{0:T(1024)(128)(4,1)} %bitcast.175), calls=%async_computation.1 | async-start | bytes 4194304 | tf_op jit(solution)/shard_map/while
  186.5 3.3 %copy-start = (f32[4,1536,128]{2,1,0:T(8,128)S(1)}, f32[4,1536,128]{2,1,0:T(8,128)}, u32[]{:S(2)}) copy-start(f32[4,1536,128]{2,1,0:T(8,128)} %get-tuple-element.275) | copy-start | bytes 9437188 | tf_op jit(solution)/shard_map/while
  190.0 2.2 copy-start.9
  224.6 3.4 %copy-start.2 = (bf16[4,4,512,128]{3,2,1,0:T(8,128)(2,1)S(1)}, bf16[4,4,512,128]{3,2,1,0:T(8,128)(2,1)}, u32[]{:S(2)}) copy-start(bf16[4,4,512,128]{3,2,1,0:T(8,128)(2,1)} %get-tuple-element.302) | copy-start | bytes 6291460 | tf_op jit(solution)/shard_map/while
  224.6 7.2 %slice-start = ((s8[6291456]{0:T(1024)(128)(4,1)}), s8[4194304]{0:T(1024)(128)(4,1)S(1)}, s32[]{:S(2)}) async-start(s8[6291456]{0:T(1024)(128)(4,1)} %bitcast.175), calls=%async_computation | async-start | bytes 8388608 | tf_op jit(solution)/shard_map/while
  228.0 3.8 %slice-start.1 = ((s8[6291456]{0:T(1024)(128)(4,1)}), s8[2097152]{0:T(1024)(128)(4,1)S(1)}, s32[]{:S(2)}) async-start(s8[6291456]{0:T(1024)(128)(4,1)} %bitcast.175), calls=%async_computation.1 | async-start | bytes 4194304 | tf_op jit(solution)/shard_map/while
  237.2 3.3 %copy-start = (f32[4,1536,128]{2,1,0:T(8,128)S(1)}, f32[4,1536,128]{2,1,0:T(8,128)}, u32[]{:S(2)}) copy-start(f32[4,1536,128]{2,1,0:T(8,128)} %get-tuple-element.275) | copy-start | bytes 9437188 | tf_op jit(solution)/shard_map/while
  240.7 2.2 copy-start.9
  248.2 30.8 %collective-permute-start.4 = (f32[512,512]{1,0:T(8,128)}, f32[512,512]{1,0:T(8,128)}, u32[]{:S(2)}, u32[]{:S(2)}) collective-permute-start(f32[512,512]{1,0:T(8,128)} %bitcast.116), channel_id=1, source_target_pairs={{1,0},{2,1},{3,2},{4,3},{5,4},{6,5},{7,6},{8,7},{9,8},{10,9},{11,1... | collective-permute-start | bytes 3145736 | tf_op jit(solution)/shard_map/ppermute | solution.py:16
  256.6 46.9 %collective-permute-start.5 = (f32[512,512]{1,0:T(8,128)}, f32[512,512]{1,0:T(8,128)}, u32[]{:S(2)}, u32[]{:S(2)}) collective-permute-start(f32[512,512]{1,0:T(8,128)} %bitcast.115), channel_id=1, source_target_pairs={{2,0},{3,1},{4,2},{5,3},{6,4},{7,5},{8,6},{9,7},{10,8},{11,9},{12,... | collective-permute-start | bytes 3145736 | tf_op jit(solution)/shard_map/ppermute | solution.py:16
  260.2 7.7 %copy-start.5 = (bf16[4,4,512,128]{3,2,1,0:T(8,128)(2,1)S(1)}, bf16[4,4,512,128]{3,2,1,0:T(8,128)(2,1)}, u32[]{:S(2)}) copy-start(bf16[4,4,512,128]{3,2,1,0:T(8,128)(2,1)} %get-tuple-element.75) | copy-start | bytes 6291460
  262.5 51.7 %collective-permute-start.6 = (f32[512,512]{1,0:T(8,128)}, f32[512,512]{1,0:T(8,128)}, u32[]{:S(2)}, u32[]{:S(2)}) collective-permute-start(f32[512,512]{1,0:T(8,128)} %bitcast.114), channel_id=1, source_target_pairs={{1,0},{2,1},{3,2},{4,3},{5,4},{6,5},{7,6},{8,7},{9,8},{10,9},{11,1... | collective-permute-start | bytes 3145736 | tf_op jit(solution)/shard_map/ppermute | solution.py:16
  264.4 63.0 %collective-permute-start.7 = (f32[512,512]{1,0:T(8,128)}, f32[512,512]{1,0:T(8,128)}, u32[]{:S(2)}, u32[]{:S(2)}) collective-permute-start(f32[512,512]{1,0:T(8,128)} %bitcast.113), channel_id=1, source_target_pairs={{2,0},{3,1},{4,2},{5,3},{6,4},{7,5},{8,6},{9,7},{10,8},{11,9},{12,... | collective-permute-start | bytes 3145736 | tf_op jit(solution)/shard_map/ppermute | solution.py:16
  275.6 27.9 %copy-start.3 = (f32[4,64,8,128]{3,2,1,0:T(8,128)S(1)}, f32[4,64,8,128]{3,2,1,0:T(8,128)}, u32[]{:S(2)}) copy-start(f32[4,64,8,128]{3,2,1,0:T(8,128)} %get-tuple-element.147) | copy-start | bytes 3145732
  278.4 49.0 %copy-start.4 = (f32[4,64,8,128]{3,2,1,0:T(8,128)S(1)}, f32[4,64,8,128]{3,2,1,0:T(8,128)}, u32[]{:S(2)}) copy-start(f32[4,64,8,128]{3,2,1,0:T(8,128)} %get-tuple-element.144) | copy-start | bytes 3145732
  (9 other events, 14.8 us)
where the time goes:
time: 332 us; the launch traced here: 330 us
  local copies, waits for them, and re-layouts  131 us (39%)
  matrix products  73.4 us (22%)
  waiting for transfers between devices  54.1 us (16%)
  starting transfers between devices  27 us (8%)
  other arithmetic  25.3 us (8%)
  loops' own time  18.4 us (6%)
    while x96, local copies, waits for them, and re-layouts  70.8 us
    ppermute x8, waiting for transfers between devices, shifted(): lax.ppermute(value, axis, [(source, source + steps) for source in range(i...  54.1 us
    sub x4, matrix products, softmax_rows(): unnormed = jnp.where(allowed, jnp.exp(masked - row_max), 0.0)  27.1 us
    ppermute x8, starting transfers between devices, shifted(): lax.ppermute(value, axis, [(source, source + steps) for source in range(i...  27 us
    another operation x1, loops' own time, per_device(): lax.scan(per_block, (zeros_acc, zeros_acc), (query_blocks, grad_blocks, b...  18.4 us
    convert_element_type x4, other arithmetic, attend_dense(): probs_low = attn_probs.astype(jnp.bfloat16)  13.5 us
    dot_general x4, matrix products, attend_dense(): jnp.einsum('hqk,hkd->hqd', grad_scores, key_tiles, preferred_element_type...  11.7 us
    reshape x4, local copies, waits for them, and re-layouts, to_blocks(): shaped = array.reshape(blocks, BLOCK, KV_HEADS, groups, HD)  10.4 us
  transfers between devices with their start and end apart: 8, of which 5 were waited for; matrix products, arithmetic and copies ran while one was open for 9% of the time, Pallas kernels for 0%

commit v1 on v0

v1 whole, which is shorter than its diff:
```python
import functools

import jax
import jax.numpy as jnp
from jax import lax
from jax.experimental import pallas as pl
from jax.experimental.pallas import tpu as pltpu
from jax.sharding import PartitionSpec as P

HD = 128
HEADS = 16
KV_HEADS = 4
GROUPS = HEADS // KV_HEADS
BLOCK = 128
R_DEV = 2
SCALING = HD ** (-0.5)
LOG2E = 1.4426950408889634
NEG = -1e30


def shifted(value, axis, steps):
    count = lax.axis_size(axis)
    initial, last = (max(0, -steps), min(count, count - steps))
    return lax.ppermute(value, axis, [(source, source + steps) for source in range(initial, last)])


def dot(a, b, dims):
    return lax.dot_general(a, b, (dims, ((), ())), preferred_element_type=jnp.float32)


def attention_kernel(
    lists,
    doc_starts,
    base,
    q_ref,
    g_ref,
    far_ref,
    near_ref,
    own_ref,
    att_ref,
    dq_ref,
    far_out,
    near_out,
    own_out,
    win,
    win_t,
    acc,
    k_sel,
    v_sel,
    kt_sel,
    vt_sel,
    *,
    blocks,
    slots,
    docs,
):
    block = pl.program_id(1)
    rows = blocks * BLOCK

    @pl.when(block == 0)
    def _():
        for part, ref in enumerate((far_ref, near_ref, own_ref)):
            for kind in range(2):
                tile = ref[kind]
                win[kind, part * rows : (part + 1) * rows] = tile
                win_t[kind, :, part * rows : (part + 1) * rows] = tile.T
        acc[...] = jnp.zeros_like(acc)

    first = base[0]
    window_base = first - R_DEV * blocks
    query_pos = (first + block) * BLOCK + lax.broadcasted_iota(jnp.int32, (1, BLOCK), 1)
    start = jnp.zeros((1, BLOCK), jnp.int32)
    for d in range(1, docs):
        start = jnp.where(query_pos >= doc_starts[d], doc_starts[d], start)
    key_iota = lax.broadcasted_iota(jnp.int32, (BLOCK, BLOCK), 0)

    offsets = []
    masks = []
    for s in range(slots):
        entry = lists[block * slots + s]
        listed = entry >= 0
        where = pl.multiple_of(jnp.where(listed, entry - window_base, 0) * BLOCK, BLOCK)
        offsets.append(where)
        span = slice(s * BLOCK, (s + 1) * BLOCK)
        k_sel[span] = win[0, pl.ds(where, BLOCK)]
        v_sel[span] = win[1, pl.ds(where, BLOCK)]
        kt_sel[:, span] = win_t[0, :, pl.ds(where, BLOCK)]
        vt_sel[:, span] = win_t[1, :, pl.ds(where, BLOCK)]
        key_pos = key_iota + jnp.where(listed, entry * BLOCK, -BLOCK)
        allowed = key_pos >= start
        if s == 0:
            allowed = allowed & (key_pos <= query_pos)
        masks.append(allowed)
    allowed = jnp.concatenate(masks, axis=0)
    allowed = jnp.concatenate([allowed] * GROUPS, axis=1)

    def stacked(ref):
        return jnp.concatenate([ref[:, h * HD : (h + 1) * HD] for h in range(GROUPS)], axis=0)

    q4 = stacked(q_ref)
    g4 = stacked(g_ref)
    scores = dot(k_sel[...], q4, ((1,), (1,)))
    scores = jnp.where(allowed, scores, NEG)
    row_max = jnp.max(scores, axis=0, keepdims=True)
    unnormed = jnp.exp2((scores - row_max) * (SCALING * LOG2E))
    total = jnp.sum(unnormed, axis=0, keepdims=True)
    probs = unnormed * (1.0 / total)
    probs_low = probs.astype(jnp.bfloat16)
    att_t = dot(vt_sel[...], probs_low, ((1,), (0,))).astype(jnp.bfloat16)
    g4t = g4.T
    delta = jnp.sum(att_t.astype(jnp.float32) * g4t.astype(jnp.float32), axis=0, keepdims=True)
    att = att_t.T
    dprobs = dot(v_sel[...], g4t, ((1,), (0,)))
    grad_scores = (probs * (dprobs - delta)).astype(jnp.bfloat16)
    dq = (dot(kt_sel[...], grad_scores, ((1,), (0,))) * SCALING).astype(jnp.bfloat16).T
    for h in range(GROUPS):
        att_ref[:, h * HD : (h + 1) * HD] = att[h * BLOCK : (h + 1) * BLOCK]
        dq_ref[:, h * HD : (h + 1) * HD] = dq[h * BLOCK : (h + 1) * BLOCK]
    dk = dot(grad_scores, q4, ((1,), (0,)))
    dv = dot(probs_low, g4, ((1,), (0,)))
    for s in range(slots):
        span = slice(s * BLOCK, (s + 1) * BLOCK)
        at = pl.ds(offsets[s], BLOCK)
        acc[0, at] = acc[0, at] + dk[span]
        acc[1, at] = acc[1, at] + dv[span]

    @pl.when(block == blocks - 1)
    def _():
        for part, ref in enumerate((far_out, near_out, own_out)):
            span = slice(part * rows, (part + 1) * rows)
            ref[0] = (acc[0, span] * SCALING).astype(ref.dtype)
            ref[1] = acc[1, span].astype(ref.dtype)


def attend(lists, doc_starts, base, queries, out_grad, far, near, own):
    blocks, slots = lists.shape
    rows = queries.shape[0]
    width = GROUPS * HD
    window = (R_DEV + 1) * rows
    q_spec = pl.BlockSpec((BLOCK, width), lambda j, b, *_: (b, j))
    kv_spec = pl.BlockSpec((2, rows, HD), lambda j, b, *_: (0, 0, j))
    kernel = functools.partial(
        attention_kernel, blocks=blocks, slots=slots, docs=doc_starts.shape[0]
    )
    return pl.pallas_call(
        kernel,
        grid_spec=pltpu.PrefetchScalarGridSpec(
            num_scalar_prefetch=3,
            grid=(KV_HEADS, blocks),
            in_specs=[q_spec, q_spec, kv_spec, kv_spec, kv_spec],
            out_specs=[q_spec, q_spec, kv_spec, kv_spec, kv_spec],
            scratch_shapes=[
                pltpu.VMEM((2, window, HD), jnp.bfloat16),
                pltpu.VMEM((2, HD, window), jnp.bfloat16),
                pltpu.VMEM((2, window, HD), jnp.float32),
                pltpu.VMEM((slots * BLOCK, HD), jnp.bfloat16),
                pltpu.VMEM((slots * BLOCK, HD), jnp.bfloat16),
                pltpu.VMEM((HD, slots * BLOCK), jnp.bfloat16),
                pltpu.VMEM((HD, slots * BLOCK), jnp.bfloat16),
            ],
        ),
        out_shape=[
            jax.ShapeDtypeStruct(queries.shape, jnp.bfloat16),
            jax.ShapeDtypeStruct(queries.shape, jnp.bfloat16),
            jax.ShapeDtypeStruct(own.shape, jnp.bfloat16),
            jax.ShapeDtypeStruct(own.shape, jnp.bfloat16),
            jax.ShapeDtypeStruct(own.shape, jnp.float32),
        ],
        compiler_params=pltpu.CompilerParams(
            dimension_semantics=("arbitrary", "arbitrary"), vmem_limit_bytes=50 << 20
        ),
        name="attend",
    )(lists.reshape(-1), doc_starts, base, queries, out_grad, far, near, own)


def per_device(queries, keys, values, out_grad, doc_starts, block_lists):
    device = lax.axis_index("ctx")
    blocks = block_lists.shape[0]
    own = jnp.stack([keys, values])
    near = shifted(own, "ctx", 1)
    far = shifted(own, "ctx", 2)
    base = (device * blocks).astype(jnp.int32).reshape(1)
    attended, grad_query, far_part, near_part, own_part = attend(
        block_lists, doc_starts, base, queries, out_grad, far, near, own
    )
    back_far = shifted(far_part, "ctx", -2)
    back_near = shifted(near_part, "ctx", -1)
    summed = own_part + back_near.astype(jnp.float32) + back_far.astype(jnp.float32)
    summed = summed.astype(jnp.bfloat16)
    return attended, grad_query, summed[0], summed[1]


def solution(mesh):
    tokens = P(("grp", "ctx"), None)
    return jax.shard_map(
        per_device,
        mesh=mesh,
        in_specs=(tokens, tokens, tokens, tokens, P("grp"), tokens),
        out_specs=(tokens, tokens, tokens, tokens),
        check_vma=False,
    )
```

time: 332 us -> 118 us (0.36)
  local copies, waits for them, and re-layouts: 131 us -> 1.13 us
  matrix products: 73.4 us -> 0 us
  Pallas kernels: 0 us -> 34.5 us
  other arithmetic: 25.3 us -> 3.33 us
  loops' own time: 18.4 us -> 0 us
  starting transfers between devices: 27 us -> 19.3 us
  waiting for transfers between devices: 54.1 us -> 58.7 us
    while x98 -> x0, local copies, waits for them, and re-layouts: 73.9 us -> none
    dot_general x20 -> x0, matrix products: 46.3 us -> none  [the longest x4 11.7 us: attend_dense(): jnp.einsum('hqk,hkd->hqd', grad_scores, key_tiles, preferred_element_type...]
    pallas_call x0 -> x1, Pallas kernels: none -> 34.5 us  [attend(): pl.pallas_call(kernel, grid_spec=pltpu.PrefetchScalarGridSpec(num_scalar_...]
    sub x4 -> x0, matrix products: 27.1 us -> none  [softmax_rows(): unnormed = jnp.where(allowed, jnp.exp(masked - row_max), 0.0)]
    reshape x8 -> x1, local copies, waits for them, and re-layouts: 20.8 us -> 0.08 us  [attend(): lists.reshape(-1)]
    another operation x1 -> x0, loops' own time: 18.4 us -> none  [per_device(): lax.scan(per_block, (zeros_acc, zeros_acc), (query_blocks, grad_blocks, b...]
    convert_element_type x6 -> x1, other arithmetic: 18.6 us -> 2.02 us  [per_device(): summed = summed.astype(jnp.bfloat16)]
    concatenate x8 -> x0, local copies, waits for them, and re-layouts: 12.7 us -> none  [the longest x4 6.39 us: per_block(): jnp.concatenate([lax.dynamic_slice_in_dim(value_window, window_index[slot...]
  transfers between devices with their start and end apart: 8 -> 4, of which waited for: 5 -> 4; matrix products, arithmetic and copies ran while one was open for 9% -> 0% of each run, Pallas kernels for 0% -> 0%
where the time goes in v1:
time: 118 us
  waiting for transfers between devices  58.7 us (50%)
  Pallas kernels  34.5 us (29%)
  starting transfers between devices  19.3 us (16%)
  other arithmetic  3.33 us (3%)
    ppermute x4, waiting for transfers between devices, shifted(): lax.ppermute(value, axis, [(source, source + steps) for source in range(i...  58.7 us
    pallas_call x1, Pallas kernels, attend(): pl.pallas_call(kernel, grid_spec=pltpu.PrefetchScalarGridSpec(num_scalar_...  34.5 us
    ppermute x4, starting transfers between devices, shifted(): lax.ppermute(value, axis, [(source, source + steps) for source in range(i...  19.3 us
  transfers between devices with their start and end apart: 4, of which 4 were waited for; matrix products, arithmetic and copies ran while one was open for 0% of the time, Pallas kernels for 0%

profile of v1, /device:TPU:22, one launch (start us, length us, event | category | flops | bytes accessed | tf_op | source)
XLA Modules:
  0.0 117.7 jit_solution(3980923947232602157)
XLA Ops:
  0.6 0.0 copy-start.3
  0.6 0.0 copy-start
  0.7 1.3 %pad_maximum_fusion.own_ref = bf16[2,512,512]{2,1,0:T(8,128)(2,1)S(1)} fusion(bf16[1,512,512]{2,1,0:T(8,128)(2,1)} %bitcast.7, bf16[1,512,512]{2,1,0:T(8,128)(2,1)} %bitcast.8), kind=kLoop, calls=%fused_computation.1 | loop fusion | flops 524288 | bytes 2097152 | tf_op jit(solution)/shard_map/stack | solution.py:179
  2.0 0.0 copy-start.1
  2.0 1.9 %collective-permute-start.1 = (bf16[2,512,512]{2,1,0:T(8,128)(2,1)S(1)}, bf16[2,512,512]{2,1,0:T(8,128)(2,1)S(1)}, u32[]{:S(2)}, u32[]{:S(2)}) collective-permute-start(bf16[2,512,512]{2,1,0:T(8,128)(2,1)S(1)} %pad_maximum_fusion.own_ref), channel_id=1, source_target_pairs={{0,1},{1,2},{2,3},{3,4},{4,5},{5,6},{6,7},{7,8},{8,9},{9,10},{10,1... | collective-permute-start | bytes 3145736 | tf_op jit(solution)/shard_map/ppermute | solution.py:24
  3.9 3.4 %collective-permute-start = (bf16[2,512,512]{2,1,0:T(8,128)(2,1)S(1)}, bf16[2,512,512]{2,1,0:T(8,128)(2,1)S(1)}, u32[]{:S(2)}, u32[]{:S(2)}) collective-permute-start(bf16[2,512,512]{2,1,0:T(8,128)(2,1)S(1)} %pad_maximum_fusion.own_ref), channel_id=1, source_target_pairs={{0,2},{1,3},{2,4},{3,5},{4,6},{5,7},{6,8},{7,9},{8,10},{9,11},{10,... | collective-permute-start | bytes 3145736 | tf_op jit(solution)/shard_map/ppermute | solution.py:24
  7.3 0.0 copy-done.3
  7.4 0.1 reshape.14.lists
  7.4 19.3 %collective-permute-done.1.near_ref = bf16[2,512,512]{2,1,0:T(8,128)(2,1)S(1)} collective-permute-done((bf16[2,512,512]{2,1,0:T(8,128)(2,1)S(1)}, bf16[2,512,512]{2,1,0:T(8,128)(2,1)S(1)}, u32[]{:S(2)}, u32[]{:S(2)}) %collective-permute-start.1) | collective-permute-done | bytes 1048608 | tf_op jit(solution)/shard_map/ppermute | solution.py:24
  26.8 0.0 copy-start.2
  26.8 5.1 %collective-permute-done.far_ref = bf16[2,512,512]{2,1,0:T(8,128)(2,1)S(1)} collective-permute-done((bf16[2,512,512]{2,1,0:T(8,128)(2,1)S(1)}, bf16[2,512,512]{2,1,0:T(8,128)(2,1)S(1)}, u32[]{:S(2)}, u32[]{:S(2)}) %collective-permute-start) | collective-permute-done | bytes 1048608 | tf_op jit(solution)/shard_map/ppermute | solution.py:24
  31.9 0.0 copy-done.1
  31.9 0.0 copy-done.2
  31.9 0.0 copy-done
  31.9 34.5 %attend.1 = (bf16[512,2048]{1,0:T(8,128)(2,1)}, bf16[512,2048]{1,0:T(8,128)(2,1)}, bf16[2,512,512]{2,1,0:T(8,128)(2,1)S(1)}, bf16[2,512,512]{2,1,0:T(8,128)(2,1)S(1)}, f32[2,512,512]{2,1,0:T(8,128)}) custom-call(s32[24]{0:T(128)S(1)} %reshape.14.lists, s32[8]{0:T(128)S(1)} %copy-done, s32[1]{0:T(128)} %bitcast.base, bf16[512,2048]{1,0:T(8,128)(2,1)} %q_ref.1, ...), custom_call_target="tpu_custom_call" | custom-call | tf_op jit(solution)/shard_map/attend/pallas_call | solution.py:145
  66.4 11.5 %collective-permute-start.2 = (bf16[2,512,512]{2,1,0:T(8,128)(2,1)S(1)}, bf16[2,512,512]{2,1,0:T(8,128)(2,1)S(1)}, u32[]{:S(2)}, u32[]{:S(2)}) collective-permute-start(bf16[2,512,512]{2,1,0:T(8,128)(2,1)S(1)} %get-tuple-element.12), channel_id=1, source_target_pairs={{1,0},{2,1},{3,2},{4,3},{5,4},{6,5},{7,6},{8,7},{9,8},{10,9},{11,1... | collective-permute-start | bytes 3145736 | tf_op jit(solution)/shard_map/ppermute | solution.py:24
  77.9 2.5 %collective-permute-start.3 = (bf16[2,512,512]{2,1,0:T(8,128)(2,1)S(1)}, bf16[2,512,512]{2,1,0:T(8,128)(2,1)S(1)}, u32[]{:S(2)}, u32[]{:S(2)}) collective-permute-start(bf16[2,512,512]{2,1,0:T(8,128)(2,1)S(1)} %get-tuple-element.13), channel_id=1, source_target_pairs={{2,0},{3,1},{4,2},{5,3},{6,4},{7,5},{8,6},{9,7},{10,8},{11,9},{12,... | collective-permute-start | bytes 3145736 | tf_op jit(solution)/shard_map/ppermute | solution.py:24
  80.3 19.7 %collective-permute-done.2 = bf16[2,512,512]{2,1,0:T(8,128)(2,1)S(1)} collective-permute-done((bf16[2,512,512]{2,1,0:T(8,128)(2,1)S(1)}, bf16[2,512,512]{2,1,0:T(8,128)(2,1)S(1)}, u32[]{:S(2)}, u32[]{:S(2)}) %collective-permute-start.2) | collective-permute-done | bytes 1048608 | tf_op jit(solution)/shard_map/ppermute | solution.py:24
  100.0 14.6 %collective-permute-done.3 = bf16[2,512,512]{2,1,0:T(8,128)(2,1)S(1)} collective-permute-done((bf16[2,512,512]{2,1,0:T(8,128)(2,1)S(1)}, bf16[2,512,512]{2,1,0:T(8,128)(2,1)S(1)}, u32[]{:S(2)}, u32[]{:S(2)}) %collective-permute-start.3) | collective-permute-done | bytes 1048608 | tf_op jit(solution)/shard_map/ppermute | solution.py:24
  114.6 2.0 %add_convert_fusion = bf16[2,512,512]{2,1,0:T(8,128)(2,1)S(1)} fusion(bf16[2,512,512]{2,1,0:T(8,128)(2,1)S(1)} %collective-permute-done.3, f32[2,512,512]{2,1,0:T(8,128)} %get-tuple-element.11, bf16[2,512,512]{2,1,0:T(8,128)(2,1)S(1)} %collective-permute-done.2), kind=kLoop, calls=%fused_computation | loop fusion | flops 2621440 | bytes 5242880 | tf_op jit(solution)/shard_map/convert_element_type | solution.py:189
  116.6 1.0 slice_bitcast_fusion
Async XLA Ops:
  0.6 6.7 %copy-start.3 = (s32[4,6]{1,0:T(4,128)S(1)}, s32[4,6]{1,0:T(4,128)}, u32[]{:S(2)}) copy-start(s32[4,6]{1,0:T(4,128)} %param.11) | copy-start | bytes 292
  0.6 31.3 %copy-start = (s32[8]{0:T(128)S(1)}, s32[8]{0:T(128)}, u32[]{:S(2)}) copy-start(s32[8]{0:T(128)} %doc_starts.1) | copy-start | bytes 100
  2.0 29.9 %copy-start.1 = (bf16[2,512,512]{2,1,0:T(8,128)(2,1)}, bf16[2,512,512]{2,1,0:T(8,128)(2,1)S(1)}, u32[]{:S(2)}) copy-start(bf16[2,512,512]{2,1,0:T(8,128)(2,1)S(1)} %pad_maximum_fusion.own_ref) | copy-start | bytes 3145732
  2.0 24.8 %collective-permute-start.1 = (bf16[2,512,512]{2,1,0:T(8,128)(2,1)S(1)}, bf16[2,512,512]{2,1,0:T(8,128)(2,1)S(1)}, u32[]{:S(2)}, u32[]{:S(2)}) collective-permute-start(bf16[2,512,512]{2,1,0:T(8,128)(2,1)S(1)} %pad_maximum_fusion.own_ref), channel_id=1, source_target_pairs={{0,1},{1,2},{2,3},{3,4},{4,5},{5,6},{6,7},{7,8},{8,9},{9,10},{10,1... | collective-permute-start | bytes 3145736 | tf_op jit(solution)/shard_map/ppermute | solution.py:24
  3.9 28.0 %collective-permute-start = (bf16[2,512,512]{2,1,0:T(8,128)(2,1)S(1)}, bf16[2,512,512]{2,1,0:T(8,128)(2,1)S(1)}, u32[]{:S(2)}, u32[]{:S(2)}) collective-permute-start(bf16[2,512,512]{2,1,0:T(8,128)(2,1)S(1)} %pad_maximum_fusion.own_ref), channel_id=1, source_target_pairs={{0,2},{1,3},{2,4},{3,5},{4,6},{5,7},{6,8},{7,9},{8,10},{9,11},{10,... | collective-permute-start | bytes 3145736 | tf_op jit(solution)/shard_map/ppermute | solution.py:24
  26.8 5.1 %copy-start.2 = (bf16[2,512,512]{2,1,0:T(8,128)(2,1)}, bf16[2,512,512]{2,1,0:T(8,128)(2,1)S(1)}, u32[]{:S(2)}) copy-start(bf16[2,512,512]{2,1,0:T(8,128)(2,1)S(1)} %collective-permute-done.1.near_ref) | copy-start | bytes 3145732
  66.4 33.6 %collective-permute-start.2 = (bf16[2,512,512]{2,1,0:T(8,128)(2,1)S(1)}, bf16[2,512,512]{2,1,0:T(8,128)(2,1)S(1)}, u32[]{:S(2)}, u32[]{:S(2)}) collective-permute-start(bf16[2,512,512]{2,1,0:T(8,128)(2,1)S(1)} %get-tuple-element.12), channel_id=1, source_target_pairs={{1,0},{2,1},{3,2},{4,3},{5,4},{6,5},{7,6},{8,7},{9,8},{10,9},{11,1... | collective-permute-start | bytes 3145736 | tf_op jit(solution)/shard_map/ppermute | solution.py:24
  77.9 36.8 %collective-permute-start.3 = (bf16[2,512,512]{2,1,0:T(8,128)(2,1)S(1)}, bf16[2,512,512]{2,1,0:T(8,128)(2,1)S(1)}, u32[]{:S(2)}, u32[]{:S(2)}) collective-permute-start(bf16[2,512,512]{2,1,0:T(8,128)(2,1)S(1)} %get-tuple-element.13), channel_id=1, source_target_pairs={{2,0},{3,1},{4,2},{5,3},{6,4},{7,5},{8,6},{9,7},{10,8},{11,9},{12,... | collective-permute-start | bytes 3145736 | tf_op jit(solution)/shard_map/ppermute | solution.py:24

commit v2 on v1

v2 whole, which is shorter than its diff:
```python
import functools

import jax
import jax.numpy as jnp
from jax import lax
from jax.experimental import pallas as pl
from jax.experimental.pallas import tpu as pltpu
from jax.sharding import PartitionSpec as P

HD = 128
HEADS = 16
KV_HEADS = 4
GROUPS = HEADS // KV_HEADS
WIDTH = GROUPS * HD
CORES = 2
PER_CORE = KV_HEADS // CORES
PARTS = 2 * CORES
BLOCK = 128
SCALING = HD ** (-0.5)
LOG2E = 1.4426950408889634
NEG = -1e30
BF16 = jnp.bfloat16
F32 = jnp.float32

ANY = pl.BlockSpec(memory_space=pltpu.HBM)
LARGE = pltpu.CompilerParams(vmem_limit_bytes=60 << 20)
SMALL = pltpu.CompilerParams(vmem_limit_bytes=16 << 20)


def dot(a, b, dims):
    return lax.dot_general(a, b, (dims, ((), ())), preferred_element_type=F32)


def columns(head, width):
    return pl.ds(pl.multiple_of(head * width, width), width)


def pack_kernel(core, keys, values, sib_keys, sib_values, out):
    rows = keys.shape[0]
    for kind, pair in enumerate(((keys, sib_keys), (values, sib_values))):
        for which in range(CORES):
            out[kind, which * rows : (which + 1) * rows] = pair[which][...]


def pack(head, core, keys, values, sib_keys, sib_values):
    rows = keys.shape[0]
    spec = pl.BlockSpec((rows, HD), lambda i, c: (0, c[0] * PER_CORE + head))
    return pl.pallas_call(
        pack_kernel,
        grid_spec=pltpu.PrefetchScalarGridSpec(
            num_scalar_prefetch=1,
            grid=(1,),
            in_specs=[spec] * 4,
            out_specs=pl.BlockSpec((2, CORES * rows, HD), lambda i, c: (0, 0, 0)),
        ),
        out_shape=jax.ShapeDtypeStruct((2, CORES * rows, HD), BF16),
        compiler_params=LARGE,
        name="pack",
    )(core, keys, values, sib_keys, sib_values)


def attention_kernel(*refs, head, blocks, slots, docs, aliased):
    lists, starts, where = refs[:3]
    refs = refs[3:]
    queries, out_grad, sib_queries, sib_out_grad, chip, prev = refs[:6]
    refs = refs[8 if aliased else 6 :]
    att_out, dq_out, returned, chip_part, prev_part = refs[:5]
    (win, win_t, acc, rows_in, rows_out, back, k_sel, v_sel, kt_sel, vt_sel, sems) = refs[5:]
    device = where[0]
    core = lax.rem(device, CORES)
    rows = blocks * BLOCK
    own_columns = columns(core * PER_CORE + head, WIDTH)

    loads = []
    for part, source in enumerate((chip, prev)):
        loads.append((source, win.at[:, part * CORES * rows : (part + 1) * CORES * rows]))
    for i, source in enumerate((queries, out_grad, sib_queries, sib_out_grad)):
        to = rows_in.at[i % 2, pl.ds(i // 2 * rows, rows)]
        loads.append((source.at[:, own_columns], to))
    loads = [pltpu.make_async_copy(a, b, sems.at[i]) for i, (a, b) in enumerate(loads)]
    for copy in loads:
        copy.start()
    acc[...] = jnp.zeros_like(acc)
    for part in range(2):
        loads[part].wait()
        span = slice(part * CORES * rows, (part + 1) * CORES * rows)
        for kind in range(2):
            win_t[kind, :, span] = win[kind, span].T
    loads[2].wait()
    loads[3].wait()

    chip_first = (device - core) * blocks

    def unit(i, is_sibling, live):
        first = (device + is_sibling * (1 - 2 * core)) * blocks
        query_block = first + i
        query_pos = query_block * BLOCK + lax.broadcasted_iota(jnp.int32, (1, BLOCK), 1)
        start = jnp.zeros((1, BLOCK), jnp.int32)
        for d in range(1, docs):
            start = jnp.where(query_pos >= starts[d], starts[d], start)
        key_iota = lax.broadcasted_iota(jnp.int32, (BLOCK, BLOCK), 0)
        offsets = []
        masks = []
        for s in range(live):
            entry = lists[(is_sibling * blocks + i) * slots + s]
            rel = entry - chip_first + CORES * blocks
            owner = lax.rem(lax.div(rel, blocks), CORES)
            part = CORES * (1 - lax.div(rel, CORES * blocks)) + (owner + core) % CORES
            at = pl.multiple_of((part * blocks + lax.rem(rel, blocks)) * BLOCK, BLOCK)
            offsets.append(at)
            span = slice(s * BLOCK, (s + 1) * BLOCK)
            k_sel[span] = win[0, pl.ds(at, BLOCK)]
            v_sel[span] = win[1, pl.ds(at, BLOCK)]
            kt_sel[:, span] = win_t[0, :, pl.ds(at, BLOCK)]
            vt_sel[:, span] = win_t[1, :, pl.ds(at, BLOCK)]
            key_pos = key_iota + entry * BLOCK
            allowed = key_pos >= start
            if s == 0:
                allowed = allowed & (key_pos <= query_pos)
            masks.append(allowed)
        allowed = jnp.concatenate(masks, axis=0)
        allowed = jnp.concatenate([allowed] * GROUPS, axis=1)

        span = slice(0, live * BLOCK)
        at = pl.ds(pl.multiple_of((is_sibling * blocks + i) * BLOCK, BLOCK), BLOCK)

        def stacked(kind):
            tiles = [rows_in[kind, at, h * HD : (h + 1) * HD] for h in range(GROUPS)]
            return jnp.concatenate(tiles, axis=0)

        q4 = stacked(0)
        g4 = stacked(1)
        scores = dot(k_sel[span], q4, ((1,), (1,)))
        scores = jnp.where(allowed, scores, NEG)
        row_max = jnp.max(scores, axis=0, keepdims=True)
        unnormed = jnp.exp2((scores - row_max) * (SCALING * LOG2E))
        total = jnp.sum(unnormed, axis=0, keepdims=True)
        probs = unnormed * (1.0 / total)
        probs_low = probs.astype(BF16)
        att_t = dot(vt_sel[:, span], probs_low, ((1,), (0,))).astype(BF16)
        g4t = g4.T
        delta = jnp.sum(att_t.astype(F32) * g4t.astype(F32), axis=0, keepdims=True)
        att = att_t.T
        dprobs = dot(v_sel[span], g4t, ((1,), (0,)))
        grad_scores = (probs * (dprobs - delta)).astype(BF16)
        dq = (dot(kt_sel[:, span], grad_scores, ((1,), (0,))) * SCALING).astype(BF16).T
        for h in range(GROUPS):
            rows_out[0, at, h * HD : (h + 1) * HD] = att[h * BLOCK : (h + 1) * BLOCK]
            rows_out[1, at, h * HD : (h + 1) * HD] = dq[h * BLOCK : (h + 1) * BLOCK]
        dk = dot(grad_scores, q4, ((1,), (0,)))
        dv = dot(probs_low, g4, ((1,), (0,)))
        for s in range(live):
            span = slice(s * BLOCK, (s + 1) * BLOCK)
            at = pl.ds(offsets[s], BLOCK)
            acc[0, at] = acc[0, at] + dk[span]
            acc[1, at] = acc[1, at] + dv[span]

    def side(is_sibling):
        def step(i, carry):
            base = (is_sibling * blocks + i) * slots
            count = jnp.int32(0)
            for s in range(slots):
                count = count + (lists[base + s] >= 0).astype(jnp.int32)
            for live in range(1, slots + 1):

                @pl.when(count == live)
                def _(live=live):
                    unit(i, is_sibling, live)

            return carry

        return step

    def both(j, carry):
        is_sibling = lax.div(j, blocks)

        @pl.when(j == blocks)
        def _():
            loads[4].wait()
            loads[5].wait()

        return side(is_sibling)(lax.rem(j, blocks), carry)

    lax.fori_loop(0, CORES * blocks, both, 0)

    stores = [
        (rows_out.at[0, :rows], att_out.at[:, own_columns]),
        (rows_out.at[1, :rows], dq_out.at[:, own_columns]),
        (rows_out.at[:, rows:], returned),
        (acc.at[:, : CORES * rows], chip_part),
        (back, prev_part),
    ]
    stores = [pltpu.make_async_copy(a, b, sems.at[i]) for i, (a, b) in enumerate(stores)]
    for copy in stores[:3]:
        copy.start()
    for kind, scale in enumerate((SCALING, 1.0)):
        back[kind] = (acc[kind, CORES * rows :] * scale).astype(BF16)
    for copy in stores[3:]:
        copy.start()
    for copy in stores:
        copy.wait()


def attend(head, lists, starts, where, arrays, full=()):
    slots = lists.shape[1]
    blocks = lists.shape[0] // CORES
    rows = blocks * BLOCK
    window = PARTS * rows
    kernel = functools.partial(
        attention_kernel,
        head=head,
        blocks=blocks,
        slots=slots,
        docs=starts.shape[0],
        aliased=bool(full),
    )
    whole = jax.ShapeDtypeStruct(arrays[0].shape, BF16)
    n_in = len(arrays) + len(full)
    return pl.pallas_call(
        kernel,
        grid_spec=pltpu.PrefetchScalarGridSpec(
            num_scalar_prefetch=3,
            grid=(),
            in_specs=[ANY] * n_in,
            out_specs=[ANY] * 5,
            scratch_shapes=[
                pltpu.VMEM((2, window, HD), BF16),
                pltpu.VMEM((2, HD, window), BF16),
                pltpu.VMEM((2, window, HD), F32),
                pltpu.VMEM((2, CORES * rows, WIDTH), BF16),
                pltpu.VMEM((2, CORES * rows, WIDTH), BF16),
                pltpu.VMEM((2, CORES * rows, HD), BF16),
                pltpu.VMEM((slots * BLOCK, HD), BF16),
                pltpu.VMEM((slots * BLOCK, HD), BF16),
                pltpu.VMEM((HD, slots * BLOCK), BF16),
                pltpu.VMEM((HD, slots * BLOCK), BF16),
                pltpu.SemaphoreType.DMA((8,)),
            ],
        ),
        out_shape=[
            whole,
            whole,
            jax.ShapeDtypeStruct((2, rows, WIDTH), BF16),
            jax.ShapeDtypeStruct((2, CORES * rows, HD), F32),
            jax.ShapeDtypeStruct((2, CORES * rows, HD), BF16),
        ],
        input_output_aliases={9: 0, 10: 1} if full else {},
        compiler_params=LARGE,
        cost_estimate=pl.CostEstimate(
            flops=10 * CORES * blocks * slots * GROUPS * BLOCK * BLOCK * HD,
            transcendentals=CORES * blocks * slots * GROUPS * BLOCK * BLOCK,
            bytes_accessed=10 << 20,
        ),
        name="attend",
    )(lists.reshape(-1), starts, where, *arrays, *full)


def place_kernel(core, *refs):
    h = pl.program_id(0)
    returned, outs = refs[:PER_CORE], refs[-2:]
    for i in range(PER_CORE):

        @pl.when(h == i)
        def _():
            for kind in range(2):
                outs[kind][...] = returned[i][kind]


def place(core, returned, full):
    rows = full[0].shape[0]
    half = rows // 2
    in_spec = pl.BlockSpec((2, half, WIDTH), lambda h, i, *_: (0, i, 0))
    out_spec = pl.BlockSpec((half, WIDTH), lambda h, i, c: (i, (1 - c[0]) * PER_CORE + h))
    return pl.pallas_call(
        place_kernel,
        grid_spec=pltpu.PrefetchScalarGridSpec(
            num_scalar_prefetch=1,
            grid=(PER_CORE, 2),
            in_specs=[in_spec] * PER_CORE + [ANY] * 2,
            out_specs=[out_spec] * 2,
        ),
        out_shape=[jax.ShapeDtypeStruct(f.shape, f.dtype) for f in full],
        input_output_aliases={1 + PER_CORE + i: i for i in range(2)},
        compiler_params=SMALL,
        name="place",
    )(core, *returned, *full)


def total_kernel(chip_part, back, own, other):
    rows = own.shape[1]
    for kind, scale in enumerate((SCALING, 1.0)):
        total = (chip_part[kind] * scale + back[kind].astype(F32)).astype(BF16)
        own[kind] = total[:rows]
        other[kind] = total[rows:]


def total(chip_part, back):
    rows = chip_part.shape[1] // CORES
    return pl.pallas_call(
        total_kernel,
        out_shape=[jax.ShapeDtypeStruct((2, rows, HD), BF16)] * CORES,
        compiler_params=SMALL,
        name="total",
    )(chip_part, back)


def grads_kernel(core, *refs):
    outs = refs[-2:]
    for h in range(PER_CORE):
        for which, owner in enumerate((core[0], 1 - core[0])):
            piece = refs[CORES * h + which]
            at = columns(owner * PER_CORE + h, HD)
            for kind in range(2):
                outs[kind][:, at] = piece[kind]


def grads(core, pieces):
    rows = pieces[0].shape[1]
    strip = pl.BlockSpec((2, rows, HD), lambda i, *_: (0, 0, 0))
    out = pl.BlockSpec((rows, KV_HEADS * HD), lambda i, *_: (0, 0))
    return pl.pallas_call(
        grads_kernel,
        grid_spec=pltpu.PrefetchScalarGridSpec(
            num_scalar_prefetch=1,
            grid=(1,),
            in_specs=[strip] * len(pieces),
            out_specs=[out, out],
        ),
        out_shape=[jax.ShapeDtypeStruct((rows, KV_HEADS * HD), BF16)] * 2,
        compiler_params=SMALL,
        name="grads",
    )(core, *pieces)


def per_device(queries, keys, values, out_grad, doc_starts, block_lists):
    device = lax.axis_index("ctx").astype(jnp.int32)
    count = lax.axis_size("ctx")
    core = lax.rem(device, CORES).reshape(1)
    where = device.reshape(1)
    chips = count // CORES

    pairs = [(2 * c + k, 2 * c + 1 - k) for c in range(chips) for k in range(CORES)]
    same = [(2 * c + k, 2 * c + 2 + k) for c in range(chips - 1) for k in range(CORES)]
    same_back = [(b, a) for a, b in same]

    def send(value, route):
        return lax.ppermute(value, "ctx", route)

    sib_keys, sib_values = send(keys, pairs), send(values, pairs)
    sib_keys, sib_values, late = lax.optimization_barrier(
        (sib_keys, sib_values, (queries, out_grad, block_lists))
    )
    sib_queries, sib_out_grad, sib_lists = [send(value, pairs) for value in late]
    lists = jnp.concatenate([block_lists, sib_lists])
    chip = [pack(h, core, keys, values, sib_keys, sib_values) for h in range(PER_CORE)]
    prev = [send(c, same) for c in chip]

    full, returned, chip_parts, backs = (), [], [], []
    for h in range(PER_CORE):
        arrays = (queries, out_grad, sib_queries, sib_out_grad, chip[h], prev[h])
        *full, to_sibling, chip_part, to_prev = attend(
            h, lists, doc_starts, where, arrays, tuple(full)
        )
        if backs:
            to_prev, to_sibling, backs[-1] = lax.optimization_barrier(
                (to_prev, to_sibling, backs[-1])
            )
        returned.append(send(to_sibling, pairs))
        chip_parts.append(chip_part)
        backs.append(send(to_prev, same_back))
    attended, grad_query = place(core, returned, full)
    attended, grad_query, backs[-1] = lax.optimization_barrier((attended, grad_query, backs[-1]))
    pieces = []
    for chip_part, back in zip(chip_parts, backs):
        own, other = total(chip_part, back)
        pieces += [own, send(other, pairs)]
    return attended, grad_query, *grads(core, pieces)


def solution(mesh):
    tokens = P(("grp", "ctx"), None)
    return jax.shard_map(
        per_device,
        mesh=mesh,
        in_specs=(tokens, tokens, tokens, tokens, P("grp"), tokens),
        out_specs=(tokens, tokens, tokens, tokens),
        check_vma=False,
    )
```

time: 118 us -> 79.3 us (0.67)
  the two profiles are of different devices: /device:TPU:22 before, /device:TPU:25 now
where the time goes in v2:
time: 79.3 us; the launch traced here: 77.9 us
  Pallas kernels  33.4 us (42%)
  waiting for transfers between devices  22.2 us (28%)
  starting transfers between devices  18.3 us (23%)
  local copies, waits for them, and re-layouts  3.22 us (4%)
    pallas_call x2, Pallas kernels, attend(): pl.pallas_call(kernel, grid_spec=pltpu.PrefetchScalarGridSpec(num_scalar_...  25.9 us
    ppermute x13, waiting for transfers between devices, send(): return lax.ppermute(value, 'ctx', route)  22.2 us
    ppermute x13, starting transfers between devices, send(): return lax.ppermute(value, 'ctx', route)  18.3 us
    pallas_call x2, Pallas kernels, pack(): pl.pallas_call(pack_kernel, grid_spec=pltpu.PrefetchScalarGridSpec(num_sc...  3.95 us
    unnamed x16, local copies, waits for them, and re-layouts  2.55 us
    pallas_call x1, Pallas kernels, place(): pl.pallas_call(place_kernel, grid_spec=pltpu.PrefetchScalarGridSpec(num_s...  2.14 us
  transfers between devices with their start and end apart: 13, of which 5 were waited for; matrix products, arithmetic and copies ran while one was open for 1% of the time, Pallas kernels for 41%

profile of v2, /device:TPU:25, one launch (start us, length us, event | category | flops | bytes accessed | tf_op | source)
XLA Modules:
  0.0 77.9 jit_solution(15985483775915019836)
XLA Ops:
  0.6 0.7 collective-permute-start
  1.4 0.1 collective-permute-start.1
  1.5 1.7 %collective-permute-done.sib_keys = bf16[512,512]{1,0:T(8,128)(2,1)S(1)} collective-permute-done((bf16[512,512]{1,0:T(8,128)(2,1)}, bf16[512,512]{1,0:T(8,128)(2,1)S(1)}, u32[]{:S(2)}, u32[]{:S(2)}) %collective-permute-start) | collective-permute-done | bytes 524320 | tf_op jit(solution)/shard_map/ppermute | solution.py:347
  3.1 0.7 collective-permute-done.1.sib_values
  3.9 0.4 collective-permute-start.3
  4.2 0.1 collective-permute-start.4
  4.4 0.3 copy-done.3
  4.7 2.0 %pack.2.refs_7_ = bf16[2,1024,128]{2,1,0:T(8,128)(2,1)} custom-call(s32[1]{0:T(128)} %bitcast.core, bf16[512,512]{1,0:T(8,128)(2,1)} %keys.3, bf16[512,512]{1,0:T(8,128)(2,1)} %values.3, bf16[512,512]{1,0:T(8,128)(2,1)} %copy-done.2, bf16[512,512]{1,0:T(8,128)(2,1)} %copy-done.3), custom_call_target="tpu_custom_call" | custom-call | tf_op jit(solution)/shard_map/pack/pallas_call | solution.py:48
  6.6 3.1 %collective-permute-start.5 = (bf16[2,1024,128]{2,1,0:T(8,128)(2,1)}, bf16[2,1024,128]{2,1,0:T(8,128)(2,1)S(1)}, u32[]{:S(2)}, u32[]{:S(2)}) collective-permute-start(bf16[2,1024,128]{2,1,0:T(8,128)(2,1)} %pack.2.refs_7_), channel_id=1, source_target_pairs={{0,2},{1,3},{2,4},{3,5},{4,6},{5,7},{6,8},{7,9},{8,10},{9,11},{10,... | collective-permute-start | bytes 1572872 | tf_op jit(solution)/shard_map/ppermute | solution.py:347
  9.8 2.0 %pack.3.refs_7_ = bf16[2,1024,128]{2,1,0:T(8,128)(2,1)} custom-call(s32[1]{0:T(128)} %bitcast.core, bf16[512,512]{1,0:T(8,128)(2,1)} %keys.3, bf16[512,512]{1,0:T(8,128)(2,1)} %values.3, bf16[512,512]{1,0:T(8,128)(2,1)} %copy-done.2, bf16[512,512]{1,0:T(8,128)(2,1)} %copy-done.3), custom_call_target="tpu_custom_call" | custom-call | tf_op jit(solution)/shard_map/pack/pallas_call | solution.py:48
  11.8 0.7 collective-permute-start.2
  12.4 1.9 %collective-permute-start.7 = (bf16[2,1024,128]{2,1,0:T(8,128)(2,1)}, bf16[2,1024,128]{2,1,0:T(8,128)(2,1)S(1)}, u32[]{:S(2)}, u32[]{:S(2)}) collective-permute-start(bf16[2,1024,128]{2,1,0:T(8,128)(2,1)} %pack.3.refs_7_), channel_id=1, source_target_pairs={{0,2},{1,3},{2,4},{3,5},{4,6},{5,7},{6,8},{7,9},{8,10},{9,11},{10,... | collective-permute-start | bytes 1572872 | tf_op jit(solution)/shard_map/ppermute | solution.py:347
  14.4 0.7 reshape.19.refs_0_
  15.0 7.7 %collective-permute-done.5.refs_8_ = bf16[2,1024,128]{2,1,0:T(8,128)(2,1)S(1)} collective-permute-done((bf16[2,1024,128]{2,1,0:T(8,128)(2,1)}, bf16[2,1024,128]{2,1,0:T(8,128)(2,1)S(1)}, u32[]{:S(2)}, u32[]{:S(2)}) %collective-permute-start.5) | collective-permute-done | bytes 524320 | tf_op jit(solution)/shard_map/ppermute | solution.py:347
  22.8 0.0 collective-permute-done.3.refs_5_
  22.8 0.8 %copy-done.7 = bf16[2,1024,128]{2,1,0:T(8,128)(2,1)} copy-done((bf16[2,1024,128]{2,1,0:T(8,128)(2,1)}, bf16[2,1024,128]{2,1,0:T(8,128)(2,1)S(1)}, u32[]{:S(2)}) %copy-start.7) | copy-done | bytes 524312
  23.5 0.7 copy-done.5
  24.2 12.9 %attend.2 = (bf16[512,2048]{1,0:T(8,128)(2,1)}, bf16[512,2048]{1,0:T(8,128)(2,1)}, bf16[2,512,512]{2,1,0:T(8,128)(2,1)}, f32[2,1024,128]{2,1,0:T(8,128)}, bf16[2,1024,128]{2,1,0:T(8,128)(2,1)}) custom-call(s32[48]{0:T(128)} %reshape.19.refs_0_, s32[8]{0:T(128)} %refs_1_.3, s32[1]{0:T(128)} %bitcast.1.refs_2_, bf16[512,2048]{1,0:T(8,128)(2,1)} %refs_3_.3, ...), custom_call_target="tpu_custom_call" | custom-call | flops 4026531840 | bytes 10485760 | tf_op jit(solution)/shard_map/attend/pallas_call | solution.py:219
  37.1 3.7 %collective-permute-start.8 = (bf16[2,1024,128]{2,1,0:T(8,128)(2,1)}, bf16[2,1024,128]{2,1,0:T(8,128)(2,1)S(1)}, u32[]{:S(2)}, u32[]{:S(2)}) collective-permute-start(bf16[2,1024,128]{2,1,0:T(8,128)(2,1)} %get-tuple-element.43), channel_id=1, source_target_pairs={{2,0},{3,1},{4,2},{5,3},{6,4},{7,5},{8,6},{9,7},{10,8},{11,9},{12,... | collective-permute-start | bytes 1572872 | tf_op jit(solution)/shard_map/ppermute | solution.py:347
  40.8 2.3 %collective-permute-start.6 = (bf16[2,512,512]{2,1,0:T(8,128)(2,1)}, bf16[2,512,512]{2,1,0:T(8,128)(2,1)S(1)}, u32[]{:S(2)}, u32[]{:S(2)}) collective-permute-start(bf16[2,512,512]{2,1,0:T(8,128)(2,1)} %get-tuple-element.38), channel_id=1, source_target_pairs={{0,1},{1,0},{2,3},{3,2},{4,5},{5,4},{6,7},{7,6},{8,9},{9,8},{10,11... | collective-permute-start | bytes 3145736 | tf_op jit(solution)/shard_map/ppermute | solution.py:347
  43.1 0.8 %copy-done.6 = bf16[2,1024,128]{2,1,0:T(8,128)(2,1)} copy-done((bf16[2,1024,128]{2,1,0:T(8,128)(2,1)}, bf16[2,1024,128]{2,1,0:T(8,128)(2,1)S(1)}, u32[]{:S(2)}) %copy-start.6) | copy-done | bytes 524312
  43.9 13.1 %attend.3 = (bf16[512,2048]{1,0:T(8,128)(2,1)}, bf16[512,2048]{1,0:T(8,128)(2,1)}, bf16[2,512,512]{2,1,0:T(8,128)(2,1)}, f32[2,1024,128]{2,1,0:T(8,128)}, bf16[2,1024,128]{2,1,0:T(8,128)(2,1)}) custom-call(s32[48]{0:T(128)} %reshape.19.refs_0_, s32[8]{0:T(128)} %refs_1_.3, s32[1]{0:T(128)} %bitcast.1.refs_2_, ...), custom_call_target="tpu_custom_call", output_to_operand_aliasing={{0}: (9, {}), {1}: (10, {})} | custom-call | flops 4026531840 | bytes 10485760 | tf_op jit(solution)/shard_map/attend/pallas_call | solution.py:219
  57.0 0.1 collective-permute-start.9
  57.1 3.3 %collective-permute-start.10 = (bf16[2,1024,128]{2,1,0:T(8,128)(2,1)}, bf16[2,1024,128]{2,1,0:T(8,128)(2,1)S(1)}, u32[]{:S(2)}, u32[]{:S(2)}) collective-permute-start(bf16[2,1024,128]{2,1,0:T(8,128)(2,1)} %get-tuple-element.49), channel_id=1, source_target_pairs={{2,0},{3,1},{4,2},{5,3},{6,4},{7,5},{8,6},{9,7},{10,8},{11,9},{12,... | collective-permute-start | bytes 1572872 | tf_op jit(solution)/shard_map/ppermute | solution.py:347
  60.4 0.1 total.2
  60.5 0.8 %collective-permute-start.11 = (bf16[2,512,128]{2,1,0:T(8,128)(2,1)S(1)}, bf16[2,512,128]{2,1,0:T(8,128)(2,1)S(1)}, u32[]{:S(2)}, u32[]{:S(2)}) collective-permute-start(bf16[2,512,128]{2,1,0:T(8,128)(2,1)S(1)} %get-tuple-element.55), channel_id=1, source_target_pairs={{0,1},{1,0},{2,3},{3,2},{4,5},{5,4},{6,7},{7,6},{8,9},{9,8},{10,11... | collective-permute-start | bytes 786440 | tf_op jit(solution)/shard_map/ppermute | solution.py:347
  61.4 2.1 %place.1 = (bf16[512,2048]{1,0:T(8,128)(2,1)}, bf16[512,2048]{1,0:T(8,128)(2,1)}) custom-call(s32[1]{0:T(128)} %bitcast.core, bf16[2,512,512]{2,1,0:T(8,128)(2,1)S(1)} %collective-permute-done.6.refs_0_, bf16[2,512,512]{2,1,0:T(8,128)(2,1)S(1)} %collective-permute-done.9.refs_1_, ...), custom_call_target="tpu_custom_call", output_to_operand_aliasing={{0}: (3, {}), {1}: (4, {})} | custom-call | tf_op jit(solution)/shard_map/place/pallas_call | solution.py:274
  63.5 10.9 %collective-permute-done.10.back = bf16[2,1024,128]{2,1,0:T(8,128)(2,1)S(1)} collective-permute-done((bf16[2,1024,128]{2,1,0:T(8,128)(2,1)}, bf16[2,1024,128]{2,1,0:T(8,128)(2,1)S(1)}, u32[]{:S(2)}, u32[]{:S(2)}) %collective-permute-start.10) | collective-permute-done | bytes 524320 | tf_op jit(solution)/shard_map/ppermute | solution.py:347
  74.4 0.1 total.3
  74.5 1.1 %collective-permute-start.12 = (bf16[2,512,128]{2,1,0:T(8,128)(2,1)S(1)}, bf16[2,512,128]{2,1,0:T(8,128)(2,1)S(1)}, u32[]{:S(2)}, u32[]{:S(2)}) collective-permute-start(bf16[2,512,128]{2,1,0:T(8,128)(2,1)S(1)} %get-tuple-element.59), channel_id=1, source_target_pairs={{0,1},{1,0},{2,3},{3,2},{4,5},{5,4},{6,7},{7,6},{8,9},{9,8},{10,11... | collective-permute-start | bytes 786440 | tf_op jit(solution)/shard_map/ppermute | solution.py:347
  75.6 1.2 %collective-permute-done.12.refs_3_ = bf16[2,512,128]{2,1,0:T(8,128)(2,1)S(1)} collective-permute-done((bf16[2,512,128]{2,1,0:T(8,128)(2,1)S(1)}, bf16[2,512,128]{2,1,0:T(8,128)(2,1)S(1)}, u32[]{:S(2)}, u32[]{:S(2)}) %collective-permute-start.12) | collective-permute-done | bytes 262176 | tf_op jit(solution)/shard_map/ppermute | solution.py:347
  76.8 1.1 %grads.1 = (bf16[512,512]{1,0:T(8,128)(2,1)}, bf16[512,512]{1,0:T(8,128)(2,1)}) custom-call(s32[1]{0:T(128)} %bitcast.core, bf16[2,512,128]{2,1,0:T(8,128)(2,1)S(1)} %get-tuple-element.54.refs_0_, bf16[2,512,128]{2,1,0:T(8,128)(2,1)S(1)} %collective-permute-done.11.refs_1_, bf16[2,512,128]{2,1,0:T(8,128)(2,1)S(1)} %get-tuple-element.58.refs_2_, ...), custom_call_target="tpu_custom_call" | custom-call | tf_op jit(solution)/shard_map/grads/pallas_call | solution.py:321
  (20 shorter events, 0.0 us)
Async XLA Ops:
  0.6 2.5 %collective-permute-start = (bf16[512,512]{1,0:T(8,128)(2,1)}, bf16[512,512]{1,0:T(8,128)(2,1)S(1)}, u32[]{:S(2)}, u32[]{:S(2)}) collective-permute-start(bf16[512,512]{1,0:T(8,128)(2,1)} %keys.3), channel_id=1, source_target_pairs={{0,1},{1,0},{2,3},{3,2},{4,5},{5,4},{6,7},{7,6},{8,9},{9,8},{10,11... | collective-permute-start | bytes 1572872 | tf_op jit(solution)/shard_map/ppermute | solution.py:347
  1.4 2.5 %collective-permute-start.1 = (bf16[512,512]{1,0:T(8,128)(2,1)}, bf16[512,512]{1,0:T(8,128)(2,1)S(1)}, u32[]{:S(2)}, u32[]{:S(2)}) collective-permute-start(bf16[512,512]{1,0:T(8,128)(2,1)} %values.3), channel_id=1, source_target_pairs={{0,1},{1,0},{2,3},{3,2},{4,5},{5,4},{6,7},{7,6},{8,9},{9,8},{10,11... | collective-permute-start | bytes 1572872 | tf_op jit(solution)/shard_map/ppermute | solution.py:347
  3.1 1.3 %copy-start.2 = (bf16[512,512]{1,0:T(8,128)(2,1)}, bf16[512,512]{1,0:T(8,128)(2,1)S(1)}, u32[]{:S(2)}) copy-start(bf16[512,512]{1,0:T(8,128)(2,1)S(1)} %collective-permute-done.sib_keys) | copy-start | bytes 1572868
  3.9 0.8 %copy-start.3 = (bf16[512,512]{1,0:T(8,128)(2,1)}, bf16[512,512]{1,0:T(8,128)(2,1)S(1)}, u32[]{:S(2)}) copy-start(bf16[512,512]{1,0:T(8,128)(2,1)S(1)} %collective-permute-done.1.sib_values) | copy-start | bytes 1572868
  3.9 18.9 %collective-permute-start.3 = (bf16[512,2048]{1,0:T(8,128)(2,1)}, bf16[512,2048]{1,0:T(8,128)(2,1)S(1)}, u32[]{:S(2)}, u32[]{:S(2)}) collective-permute-start(bf16[512,2048]{1,0:T(8,128)(2,1)} %refs_3_.3), channel_id=1, source_target_pairs={{0,1},{1,0},{2,3},{3,2},{4,5},{5,4},{6,7},{7,6},{8,9},{9,8},{10,11... | collective-permute-start | bytes 6291464 | tf_op jit(solution)/shard_map/ppermute | solution.py:347
  4.2 18.5 %collective-permute-start.4 = (bf16[512,2048]{1,0:T(8,128)(2,1)}, bf16[512,2048]{1,0:T(8,128)(2,1)}, u32[]{:S(2)}, u32[]{:S(2)}) collective-permute-start(bf16[512,2048]{1,0:T(8,128)(2,1)} %refs_4_.3), channel_id=1, source_target_pairs={{0,1},{1,0},{2,3},{3,2},{4,5},{5,4},{6,7},{7,6},{8,9},{9,8},{10,11... | collective-permute-start | bytes 6291464 | tf_op jit(solution)/shard_map/ppermute | solution.py:347
  4.7 7.1 %copy-start.4 = (s32[4,6]{1,0:T(4,128)S(1)}, s32[4,6]{1,0:T(4,128)}, u32[]{:S(2)}) copy-start(s32[4,6]{1,0:T(4,128)} %param.11) | copy-start | bytes 292
  6.6 16.1 %collective-permute-start.5 = (bf16[2,1024,128]{2,1,0:T(8,128)(2,1)}, bf16[2,1024,128]{2,1,0:T(8,128)(2,1)S(1)}, u32[]{:S(2)}, u32[]{:S(2)}) collective-permute-start(bf16[2,1024,128]{2,1,0:T(8,128)(2,1)} %pack.2.refs_7_), channel_id=1, source_target_pairs={{0,2},{1,3},{2,4},{3,5},{4,6},{5,7},{6,8},{7,9},{8,10},{9,11},{10,... | collective-permute-start | bytes 1572872 | tf_op jit(solution)/shard_map/ppermute | solution.py:347
  11.8 2.6 %collective-permute-start.2 = (s32[4,6]{1,0:T(4,128)S(1)}, s32[4,6]{1,0:T(4,128)S(1)}, u32[]{:S(2)}, u32[]{:S(2)}) collective-permute-start(s32[4,6]{1,0:T(4,128)S(1)} %copy-done.4), channel_id=1, source_target_pairs={{0,1},{1,0},{2,3},{3,2},{4,5},{5,4},{6,7},{7,6},{8,9},{9,8},{10,11... | collective-permute-start | bytes 296 | tf_op jit(solution)/shard_map/ppermute | solution.py:347
  12.4 30.7 %collective-permute-start.7 = (bf16[2,1024,128]{2,1,0:T(8,128)(2,1)}, bf16[2,1024,128]{2,1,0:T(8,128)(2,1)S(1)}, u32[]{:S(2)}, u32[]{:S(2)}) collective-permute-start(bf16[2,1024,128]{2,1,0:T(8,128)(2,1)} %pack.3.refs_7_), channel_id=1, source_target_pairs={{0,2},{1,3},{2,4},{3,5},{4,6},{5,7},{6,8},{7,9},{8,10},{9,11},{10,... | collective-permute-start | bytes 1572872 | tf_op jit(solution)/shard_map/ppermute | solution.py:347
  22.7 0.8 %copy-start.7 = (bf16[2,1024,128]{2,1,0:T(8,128)(2,1)}, bf16[2,1024,128]{2,1,0:T(8,128)(2,1)S(1)}, u32[]{:S(2)}) copy-start(bf16[2,1024,128]{2,1,0:T(8,128)(2,1)S(1)} %collective-permute-done.5.refs_8_) | copy-start | bytes 1572868
  22.8 1.5 %copy-start.5 = (bf16[512,2048]{1,0:T(8,128)(2,1)}, bf16[512,2048]{1,0:T(8,128)(2,1)S(1)}, u32[]{:S(2)}) copy-start(bf16[512,2048]{1,0:T(8,128)(2,1)S(1)} %collective-permute-done.3.refs_5_) | copy-start | bytes 6291460
  37.1 19.9 %collective-permute-start.8 = (bf16[2,1024,128]{2,1,0:T(8,128)(2,1)}, bf16[2,1024,128]{2,1,0:T(8,128)(2,1)S(1)}, u32[]{:S(2)}, u32[]{:S(2)}) collective-permute-start(bf16[2,1024,128]{2,1,0:T(8,128)(2,1)} %get-tuple-element.43), channel_id=1, source_target_pairs={{2,0},{3,1},{4,2},{5,3},{6,4},{7,5},{8,6},{9,7},{10,8},{11,9},{12,... | collective-permute-start | bytes 1572872 | tf_op jit(solution)/shard_map/ppermute | solution.py:347
  40.8 20.6 %collective-permute-start.6 = (bf16[2,512,512]{2,1,0:T(8,128)(2,1)}, bf16[2,512,512]{2,1,0:T(8,128)(2,1)S(1)}, u32[]{:S(2)}, u32[]{:S(2)}) collective-permute-start(bf16[2,512,512]{2,1,0:T(8,128)(2,1)} %get-tuple-element.38), channel_id=1, source_target_pairs={{0,1},{1,0},{2,3},{3,2},{4,5},{5,4},{6,7},{7,6},{8,9},{9,8},{10,11... | collective-permute-start | bytes 3145736 | tf_op jit(solution)/shard_map/ppermute | solution.py:347
  43.1 0.8 %copy-start.6 = (bf16[2,1024,128]{2,1,0:T(8,128)(2,1)}, bf16[2,1024,128]{2,1,0:T(8,128)(2,1)S(1)}, u32[]{:S(2)}) copy-start(bf16[2,1024,128]{2,1,0:T(8,128)(2,1)S(1)} %collective-permute-done.7.refs_8_) | copy-start | bytes 1572868
  43.9 16.5 %copy-start.1 = (f32[2,1024,128]{2,1,0:T(8,128)S(1)}, f32[2,1024,128]{2,1,0:T(8,128)}, u32[]{:S(2)}) copy-start(f32[2,1024,128]{2,1,0:T(8,128)} %get-tuple-element.52.chip_part) | copy-start | bytes 3145732
  57.0 4.4 %collective-permute-start.9 = (bf16[2,512,512]{2,1,0:T(8,128)(2,1)}, bf16[2,512,512]{2,1,0:T(8,128)(2,1)S(1)}, u32[]{:S(2)}, u32[]{:S(2)}) collective-permute-start(bf16[2,512,512]{2,1,0:T(8,128)(2,1)} %get-tuple-element.44), channel_id=1, source_target_pairs={{0,1},{1,0},{2,3},{3,2},{4,5},{5,4},{6,7},{7,6},{8,9},{9,8},{10,11... | collective-permute-start | bytes 3145736 | tf_op jit(solution)/shard_map/ppermute | solution.py:347
  57.1 17.3 %collective-permute-start.10 = (bf16[2,1024,128]{2,1,0:T(8,128)(2,1)}, bf16[2,1024,128]{2,1,0:T(8,128)(2,1)S(1)}, u32[]{:S(2)}, u32[]{:S(2)}) collective-permute-start(bf16[2,1024,128]{2,1,0:T(8,128)(2,1)} %get-tuple-element.49), channel_id=1, source_target_pairs={{2,0},{3,1},{4,2},{5,3},{6,4},{7,5},{8,6},{9,7},{10,8},{11,9},{12,... | collective-permute-start | bytes 1572872 | tf_op jit(solution)/shard_map/ppermute | solution.py:347
  60.5 15.1 %collective-permute-start.11 = (bf16[2,512,128]{2,1,0:T(8,128)(2,1)S(1)}, bf16[2,512,128]{2,1,0:T(8,128)(2,1)S(1)}, u32[]{:S(2)}, u32[]{:S(2)}) collective-permute-start(bf16[2,512,128]{2,1,0:T(8,128)(2,1)S(1)} %get-tuple-element.55), channel_id=1, source_target_pairs={{0,1},{1,0},{2,3},{3,2},{4,5},{5,4},{6,7},{7,6},{8,9},{9,8},{10,11... | collective-permute-start | bytes 786440 | tf_op jit(solution)/shard_map/ppermute | solution.py:347
  61.4 13.1 %copy-start = (f32[2,1024,128]{2,1,0:T(8,128)S(1)}, f32[2,1024,128]{2,1,0:T(8,128)}, u32[]{:S(2)}) copy-start(f32[2,1024,128]{2,1,0:T(8,128)} %get-tuple-element.56.chip_part) | copy-start | bytes 3145732
  74.5 2.2 %collective-permute-start.12 = (bf16[2,512,128]{2,1,0:T(8,128)(2,1)S(1)}, bf16[2,512,128]{2,1,0:T(8,128)(2,1)S(1)}, u32[]{:S(2)}, u32[]{:S(2)}) collective-permute-start(bf16[2,512,128]{2,1,0:T(8,128)(2,1)S(1)} %get-tuple-element.59), channel_id=1, source_target_pairs={{0,1},{1,0},{2,3},{3,2},{4,5},{5,4},{6,7},{7,6},{8,9},{9,8},{10,11... | collective-permute-start | bytes 786440 | tf_op jit(solution)/shard_map/ppermute | solution.py:347

commit v3 on v2

--- a/solution.py
+++ b/solution.py
@@ -23,7 +23,7 @@
 F32 = jnp.float32
 
 ANY = pl.BlockSpec(memory_space=pltpu.HBM)
-LARGE = pltpu.CompilerParams(vmem_limit_bytes=60 << 20)
+VMEM = pl.BlockSpec(memory_space=pltpu.VMEM)
 SMALL = pltpu.CompilerParams(vmem_limit_bytes=16 << 20)
 
 
@@ -35,59 +35,63 @@
     return pl.ds(pl.multiple_of(head * width, width), width)
 
 
-def pack_kernel(core, keys, values, sib_keys, sib_values, out):
+def pack_kernel(core, keys, values, *outs):
+    for h in range(PER_CORE):
+        for which, owner in enumerate((core[0], 1 - core[0])):
+            at = columns(owner * PER_CORE + h, HD)
+            for kind, source in enumerate((keys, values)):
+                outs[CORES * h + which][kind] = source[:, at]
+
+
+def pack(core, keys, values):
     rows = keys.shape[0]
-    for kind, pair in enumerate(((keys, sib_keys), (values, sib_values))):
-        for which in range(CORES):
-            out[kind, which * rows : (which + 1) * rows] = pair[which][...]
-
-
-def pack(head, core, keys, values, sib_keys, sib_values):
-    rows = keys.shape[0]
-    spec = pl.BlockSpec((rows, HD), lambda i, c: (0, c[0] * PER_CORE + head))
+    whole = pl.BlockSpec(keys.shape, lambda i, *_: (0, 0))
+    strip = pl.BlockSpec((2, rows, HD), lambda i, *_: (0, 0, 0))
     return pl.pallas_call(
         pack_kernel,
         grid_spec=pltpu.PrefetchScalarGridSpec(
             num_scalar_prefetch=1,
             grid=(1,),
-            in_specs=[spec] * 4,
-            out_specs=pl.BlockSpec((2, CORES * rows, HD), lambda i, c: (0, 0, 0)),
+            in_specs=[whole, whole],
+            out_specs=[strip] * (CORES * PER_CORE),
         ),
-        out_shape=jax.ShapeDtypeStruct((2, CORES * rows, HD), BF16),
-        compiler_params=LARGE,
+        out_shape=[jax.ShapeDtypeStruct((2, rows, HD), BF16)] * (CORES * PER_CORE),
+        compiler_params=SMALL,
         name="pack",
-    )(core, keys, values, sib_keys, sib_values)
-
-
-def attention_kernel(*refs, head, blocks, slots, docs, aliased):
+    )(core, *[pltpu.with_memory_space_constraint(a, pltpu.HBM) for a in (keys, values)])
+
+
+def attention_kernel(*refs, head, blocks, slots, docs, n_prev, n_full):
     lists, starts, where = refs[:3]
     refs = refs[3:]
-    queries, out_grad, sib_queries, sib_out_grad, chip, prev = refs[:6]
-    refs = refs[8 if aliased else 6 :]
-    att_out, dq_out, returned, chip_part, prev_part = refs[:5]
-    (win, win_t, acc, rows_in, rows_out, back, k_sel, v_sel, kt_sel, vt_sel, sems) = refs[5:]
+    row_sources, (own, sib), prev = refs[:4], refs[4:6], refs[6 : 6 + n_prev]
+    refs = refs[6 + n_prev + n_full :]
+    att_out, dq_out, returned = refs[:3]
+    parts_out, scratch = refs[3:-11], refs[-11:]
+    win, win_t, acc, rows_in, rows_out, k_sel, v_sel, kt_sel, vt_sel, in_sems, out_sem = scratch
     device = where[0]
     core = lax.rem(device, CORES)
     rows = blocks * BLOCK
     own_columns = columns(core * PER_CORE + head, WIDTH)
 
-    loads = []
-    for part, source in enumerate((chip, prev)):
-        loads.append((source, win.at[:, part * CORES * rows : (part + 1) * CORES * rows]))
-    for i, source in enumerate((queries, out_grad, sib_queries, sib_out_grad)):
-        to = rows_in.at[i % 2, pl.ds(i // 2 * rows, rows)]
-        loads.append((source.at[:, own_columns], to))
-    loads = [pltpu.make_async_copy(a, b, sems.at[i]) for i, (a, b) in enumerate(loads)]
-    for copy in loads:
-        copy.start()
+    def row_load(kind, j):
+        first, second = row_sources[kind], row_sources[2 + kind]
+        source = (first if j < blocks else second).at[pl.ds(j % blocks * BLOCK, BLOCK), own_columns]
+        to = rows_in.at[kind, j * BLOCK : (j + 1) * BLOCK]
+        return pltpu.make_async_copy(source, to, in_sems.at[kind, j])
+
+    for j in range(CORES * blocks):
+        for kind in range(2):
+            row_load(kind, j).start()
     acc[...] = jnp.zeros_like(acc)
-    for part in range(2):
-        loads[part].wait()
-        span = slice(part * CORES * rows, (part + 1) * CORES * rows)
+    at = 0
+    for source in (own, sib, *prev):
+        size = source.shape[1]
         for kind in range(2):
-            win_t[kind, :, span] = win[kind, span].T
-    loads[2].wait()
-    loads[3].wait()
+            tile = source[kind]
+            win[kind, at : at + size] = tile
+            win_t[kind, :, at : at + size] = tile.T
+        at += size
 
     chip_first = (device - core) * blocks
 
@@ -134,21 +138,22 @@
         scores = jnp.where(allowed, scores, NEG)
         row_max = jnp.max(scores, axis=0, keepdims=True)
         unnormed = jnp.exp2((scores - row_max) * (SCALING * LOG2E))
-        total = jnp.sum(unnormed, axis=0, keepdims=True)
-        probs = unnormed * (1.0 / total)
-        probs_low = probs.astype(BF16)
-        att_t = dot(vt_sel[:, span], probs_low, ((1,), (0,))).astype(BF16)
+        inverse = 1.0 / jnp.sum(unnormed, axis=0, keepdims=True)
+        low = unnormed.astype(BF16)
+        att_t = (dot(vt_sel[:, span], low, ((1,), (0,))) * inverse).astype(BF16)
         g4t = g4.T
-        delta = jnp.sum(att_t.astype(F32) * g4t.astype(F32), axis=0, keepdims=True)
+        g4t_full = g4t.astype(F32)
+        delta = jnp.sum(att_t.astype(F32) * g4t_full, axis=0, keepdims=True)
         att = att_t.T
         dprobs = dot(v_sel[span], g4t, ((1,), (0,)))
-        grad_scores = (probs * (dprobs - delta)).astype(BF16)
+        grad_scores = (low.astype(F32) * ((dprobs - delta) * inverse)).astype(BF16)
         dq = (dot(kt_sel[:, span], grad_scores, ((1,), (0,))) * SCALING).astype(BF16).T
+        g4_scaled = (g4t_full * inverse).astype(BF16).T
         for h in range(GROUPS):
             rows_out[0, at, h * HD : (h + 1) * HD] = att[h * BLOCK : (h + 1) * BLOCK]
             rows_out[1, at, h * HD : (h + 1) * HD] = dq[h * BLOCK : (h + 1) * BLOCK]
         dk = dot(grad_scores, q4, ((1,), (0,)))
-        dv = dot(probs_low, g4, ((1,), (0,)))
+        dv = dot(low, g4_scaled, ((1,), (0,)))
         for s in range(live):
             span = slice(s * BLOCK, (s + 1) * BLOCK)
             at = pl.ds(offsets[s], BLOCK)
@@ -173,35 +178,39 @@
 
     def both(j, carry):
         is_sibling = lax.div(j, blocks)
-
-        @pl.when(j == blocks)
+        i = lax.rem(j, blocks)
+        at = pl.ds(pl.multiple_of(j * BLOCK, BLOCK), BLOCK)
+        to = pl.ds(pl.multiple_of(i * BLOCK, BLOCK), BLOCK)
+        for kind in range(2):
+            landed = rows_in.at[kind, at]
+            pltpu.make_async_copy(landed, landed, in_sems.at[kind, j]).wait()
+        side(is_sibling)(i, carry)
+
+        @pl.when(j < blocks)
         def _():
-            loads[4].wait()
-            loads[5].wait()
-
-        return side(is_sibling)(lax.rem(j, blocks), carry)
+            for kind, out in enumerate((att_out, dq_out)):
+                done = rows_out.at[kind, at]
+                pltpu.make_async_copy(done, out.at[to, own_columns], out_sem).start()
+
+        @pl.when(j >= blocks)
+        def _():
+            pltpu.make_async_copy(rows_out.at[:, at], returned.at[:, to], out_sem).start()
+
+        return carry
 
     lax.fori_loop(0, CORES * blocks, both, 0)
 
-    stores = [
-        (rows_out.at[0, :rows], att_out.at[:, own_columns]),
-        (rows_out.at[1, :rows], dq_out.at[:, own_columns]),
-        (rows_out.at[:, rows:], returned),
-        (acc.at[:, : CORES * rows], chip_part),
-        (back, prev_part),
-    ]
-    stores = [pltpu.make_async_copy(a, b, sems.at[i]) for i, (a, b) in enumerate(stores)]
-    for copy in stores[:3]:
-        copy.start()
-    for kind, scale in enumerate((SCALING, 1.0)):
-        back[kind] = (acc[kind, CORES * rows :] * scale).astype(BF16)
-    for copy in stores[3:]:
-        copy.start()
-    for copy in stores:
-        copy.wait()
-
-
-def attend(head, lists, starts, where, arrays, full=()):
+    at = 0
+    for out in parts_out:
+        size = out.shape[1]
+        for kind, scale in enumerate((SCALING, 1.0)):
+            tile = acc[kind, at : at + size]
+            out[kind] = (tile * scale).astype(BF16) if out.dtype == BF16 else tile
+        at += size
+    pltpu.make_async_copy(rows_out, rows_out, out_sem).wait()
+
+
+def attend(head, lists, starts, where, arrays, full, parts):
     slots = lists.shape[1]
     blocks = lists.shape[0] // CORES
     rows = blocks * BLOCK
@@ -212,47 +221,49 @@
         blocks=blocks,
         slots=slots,
         docs=starts.shape[0],
-        aliased=bool(full),
+        n_prev=len(arrays) - 6,
+        n_full=len(full),
     )
     whole = jax.ShapeDtypeStruct(arrays[0].shape, BF16)
-    n_in = len(arrays) + len(full)
+    outs = [jax.ShapeDtypeStruct((2, n * rows, HD), kind) for n, kind in parts]
     return pl.pallas_call(
         kernel,
         grid_spec=pltpu.PrefetchScalarGridSpec(
             num_scalar_prefetch=3,
             grid=(),
-            in_specs=[ANY] * n_in,
-            out_specs=[ANY] * 5,
+            in_specs=[ANY] * 4 + [VMEM] * (len(arrays) - 4) + [ANY] * len(full),
+            out_specs=[ANY] * 3 + [VMEM] * len(outs),
             scratch_shapes=[
                 pltpu.VMEM((2, window, HD), BF16),
                 pltpu.VMEM((2, HD, window), BF16),
                 pltpu.VMEM((2, window, HD), F32),
                 pltpu.VMEM((2, CORES * rows, WIDTH), BF16),
                 pltpu.VMEM((2, CORES * rows, WIDTH), BF16),
-                pltpu.VMEM((2, CORES * rows, HD), BF16),
                 pltpu.VMEM((slots * BLOCK, HD), BF16),
                 pltpu.VMEM((slots * BLOCK, HD), BF16),
                 pltpu.VMEM((HD, slots * BLOCK), BF16),
                 pltpu.VMEM((HD, slots * BLOCK), BF16),
-                pltpu.SemaphoreType.DMA((8,)),
+                pltpu.SemaphoreType.DMA((2, CORES * blocks)),
+                pltpu.SemaphoreType.DMA,
             ],
         ),
-        out_shape=[
-            whole,
-            whole,
-            jax.ShapeDtypeStruct((2, rows, WIDTH), BF16),
-            jax.ShapeDtypeStruct((2, CORES * rows, HD), F32),
-            jax.ShapeDtypeStruct((2, CORES * rows, HD), BF16),
-        ],
-        input_output_aliases={9: 0, 10: 1} if full else {},
-        compiler_params=LARGE,
+        out_shape=[whole, whole, jax.ShapeDtypeStruct((2, rows, WIDTH), BF16), *outs],
+        input_output_aliases={3 + len(arrays) + i: i for i in range(len(full))},
+        compiler_params=pltpu.CompilerParams(vmem_limit_bytes=40 << 20),
         cost_estimate=pl.CostEstimate(
             flops=10 * CORES * blocks * slots * GROUPS * BLOCK * BLOCK * HD,
             transcendentals=CORES * blocks * slots * GROUPS * BLOCK * BLOCK,
             bytes_accessed=10 << 20,
         ),
         name="attend",
-    )(lists.reshape(-1), starts, where, *arrays, *full)
+    )(
+        lists.reshape(-1),
+        starts,
+        where,
+        *[pltpu.with_memory_space_constraint(a, pltpu.HBM) for a in arrays[:2]],
+        *arrays[2:],
+        *full,
+    )
 
 
 def place_kernel(core, *refs):
@@ -306,12 +317,19 @@
 
 def grads_kernel(core, *refs):
     outs = refs[-2:]
-    for h in range(PER_CORE):
+    pieces = refs[:-2]
+    own_part, own_back, other_part, other_back = pieces[-4:]
+    for kind, scale in enumerate((SCALING, 1.0)):
         for which, owner in enumerate((core[0], 1 - core[0])):
-            piece = refs[CORES * h + which]
-            at = columns(owner * PER_CORE + h, HD)
-            for kind in range(2):
-                outs[kind][:, at] = piece[kind]
+            for h in range(PER_CORE - 1):
+                at = columns(owner * PER_CORE + h, HD)
+                outs[kind][:, at] = pieces[CORES * h + which][kind]
+        at = columns(core[0] * PER_CORE + PER_CORE - 1, HD)
+        value = own_part[kind] * scale + own_back[kind].astype(F32)
+        outs[kind][:, at] = value.astype(BF16)
+        at = columns((1 - core[0]) * PER_CORE + PER_CORE - 1, HD)
+        value = other_part[kind].astype(F32) + other_back[kind].astype(F32)
+        outs[kind][:, at] = value.astype(BF16)
 
 
 def grads(core, pieces):
@@ -341,39 +359,47 @@
 
     pairs = [(2 * c + k, 2 * c + 1 - k) for c in range(chips) for k in range(CORES)]
     same = [(2 * c + k, 2 * c + 2 + k) for c in range(chips - 1) for k in range(CORES)]
+    cross = [(2 * c + k, 2 * c + 3 - k) for c in range(chips - 1) for k in range(CORES)]
     same_back = [(b, a) for a, b in same]
+    cross_back = [(b, a) for a, b in cross]
 
     def send(value, route):
         return lax.ppermute(value, "ctx", route)
 
-    sib_keys, sib_values = send(keys, pairs), send(values, pairs)
-    sib_keys, sib_values, late = lax.optimization_barrier(
-        (sib_keys, sib_values, (queries, out_grad, block_lists))
-    )
-    sib_queries, sib_out_grad, sib_lists = [send(value, pairs) for value in late]
-    lists = jnp.concatenate([block_lists, sib_lists])
-    chip = [pack(h, core, keys, values, sib_keys, sib_values) for h in range(PER_CORE)]
-    prev = [send(c, same) for c in chip]
-
-    full, returned, chip_parts, backs = (), [], [], []
+    packed = pack(core, keys, values)
+    own, other, sib, prev = packed[0::CORES], packed[1::CORES], [], []
     for h in range(PER_CORE):
-        arrays = (queries, out_grad, sib_queries, sib_out_grad, chip[h], prev[h])
-        *full, to_sibling, chip_part, to_prev = attend(
-            h, lists, doc_starts, where, arrays, tuple(full)
-        )
-        if backs:
-            to_prev, to_sibling, backs[-1] = lax.optimization_barrier(
-                (to_prev, to_sibling, backs[-1])
-            )
+        mine, theirs = own[h], other[h]
+        sib.append(send(theirs, pairs))
+        if h == 0:
+            prev.append([send(mine, same), send(theirs, cross)])
+        else:
+            prev.append([send(jnp.concatenate([mine, sib[h]], axis=1), same)])
+    sib_queries, sib_out_grad = send(queries, pairs), send(out_grad, pairs)
+    lists = jnp.concatenate([block_lists, send(block_lists, pairs)])
+
+    full, returned, pieces, back = (), [], [], None
+    for h in range(PER_CORE):
+        last = h == PER_CORE - 1
+        parts = [(1, F32)] + [(1, BF16)] * 3 if last else [(CORES, F32), (CORES, BF16)]
+        arrays = (queries, out_grad, sib_queries, sib_out_grad, own[h], sib[h], *prev[h])
+        att, dq, to_sibling, *parts = attend(h, lists, doc_starts, where, arrays, full, parts)
+        full = (att, dq)
+        if h > 0:
+            to_sibling, parts, back = lax.optimization_barrier((to_sibling, parts, back))
+            own_total, other_total = total(chip_part, back)
+            pieces += [own_total, send(other_total, pairs)]
         returned.append(send(to_sibling, pairs))
-        chip_parts.append(chip_part)
-        backs.append(send(to_prev, same_back))
+        if not last:
+            chip_part, to_prev = parts
+            back = send(to_prev, same_back)
+        else:
+            own_part, sib_part, to_same, to_cross = parts
+            own_back, other_back = send(to_same, same_back), send(to_cross, cross_back)
+            other_part = send(sib_part, pairs)
     attended, grad_query = place(core, returned, full)
-    attended, grad_query, backs[-1] = lax.optimization_barrier((attended, grad_query, backs[-1]))
-    pieces = []
-    for chip_part, back in zip(chip_parts, backs):
-        own, other = total(chip_part, back)
-        pieces += [own, send(other, pairs)]
+    attended, grad_query, other_back = lax.optimization_barrier((attended, grad_query, other_back))
+    pieces += [own_part, own_back, other_part, other_back]
     return attended, grad_query, *grads(core, pieces)
 
 

time: 79.3 us -> 69.7 us (0.88)
  the two profiles are of different devices: /device:TPU:25 before, /device:TPU:22 now
where the time goes in v3:
time: 69.7 us; the launch traced here: 69.6 us
  Pallas kernels  33.6 us (48%)
  starting transfers between devices  20.2 us (29%)
  waiting for transfers between devices  14.2 us (20%)
  between operations  0.77 us (1%)
  other arithmetic  0.72 us (1%)
    pallas_call x2, Pallas kernels, attend(): pl.pallas_call(kernel, grid_spec=pltpu.PrefetchScalarGridSpec(num_scalar_...  28.9 us
    ppermute x15, starting transfers between devices, send(): return lax.ppermute(value, 'ctx', route)  20.2 us
    ppermute x15, waiting for transfers between devices, send(): return lax.ppermute(value, 'ctx', route)  14.2 us
    pallas_call x1, Pallas kernels, place(): pl.pallas_call(place_kernel, grid_spec=pltpu.PrefetchScalarGridSpec(num_s...  2.1 us
  transfers between devices with their start and end apart: 15, of which 6 were waited for; matrix products, arithmetic and copies ran while one was open for 1% of the time, Pallas kernels for 47%

profile of v3, /device:TPU:22, one launch (start us, length us, event | category | flops | bytes accessed | tf_op | source)
XLA Modules:
  0.0 69.6 jit_solution(109088719582319282)
XLA Ops:
  0.6 0.1 collective-permute-start.1
  0.7 0.5 collective-permute-start.2
  1.2 1.4 %pack.1 = (bf16[2,512,128]{2,1,0:T(8,128)(2,1)S(1)}, bf16[2,512,128]{2,1,0:T(8,128)(2,1)S(1)}, bf16[2,512,128]{2,1,0:T(8,128)(2,1)S(1)}, bf16[2,512,128]{2,1,0:T(8,128)(2,1)S(1)}) custom-call(s32[1]{0:T(128)} %bitcast.core, bf16[512,512]{1,0:T(8,128)(2,1)} %keys.1, bf16[512,512]{1,0:T(8,128)(2,1)} %values.1), custom_call_target="tpu_custom_call" | custom-call | tf_op jit(solution)/shard_map/pack/pallas_call | solution.py:50
  2.6 0.1 collective-permute-start.7
  2.7 0.4 collective-permute-start
  3.2 3.4 %collective-permute-start.4 = (bf16[2,512,128]{2,1,0:T(8,128)(2,1)S(1)}, bf16[2,512,128]{2,1,0:T(8,128)(2,1)S(1)}, u32[]{:S(2)}, u32[]{:S(2)}) collective-permute-start(bf16[2,512,128]{2,1,0:T(8,128)(2,1)S(1)} %get-tuple-element.35.refs_7_), channel_id=1, source_target_pairs={{0,2},{1,3},{2,4},{3,5},{4,6},{5,7},{6,8},{7,9},{8,10},{9,11},{10,... | collective-permute-start | bytes 786440 | tf_op jit(solution)/shard_map/ppermute | solution.py:367
  6.6 0.7 collective-permute-done
  7.3 3.2 %collective-permute-start.5 = (bf16[2,512,128]{2,1,0:T(8,128)(2,1)S(1)}, bf16[2,512,128]{2,1,0:T(8,128)(2,1)}, u32[]{:S(2)}, u32[]{:S(2)}) collective-permute-start(bf16[2,512,128]{2,1,0:T(8,128)(2,1)S(1)} %get-tuple-element.36), channel_id=1, source_target_pairs={{0,3},{1,2},{2,5},{3,4},{4,7},{5,6},{6,9},{7,8},{8,11},{9,10},{10,... | collective-permute-start | bytes 786440 | tf_op jit(solution)/shard_map/ppermute | solution.py:367
  10.4 0.0 collective-permute-done.7.refs_8_
  10.5 0.4 collective-permute-start.3
  10.9 0.7 pad_add_fusion
  11.6 0.1 reshape.19.refs_0_
  11.7 2.5 %collective-permute-done.4.refs_9_ = bf16[2,512,128]{2,1,0:T(8,128)(2,1)S(1)} collective-permute-done((bf16[2,512,128]{2,1,0:T(8,128)(2,1)S(1)}, bf16[2,512,128]{2,1,0:T(8,128)(2,1)S(1)}, u32[]{:S(2)}, u32[]{:S(2)}) %collective-permute-start.4) | collective-permute-done | bytes 262176 | tf_op jit(solution)/shard_map/ppermute | solution.py:367
  14.2 4.3 %collective-permute-start.8 = (bf16[2,1024,128]{2,1,0:T(8,128)(2,1)S(1)}, bf16[2,1024,128]{2,1,0:T(8,128)(2,1)S(1)}, u32[]{:S(2)}, u32[]{:S(2)}) collective-permute-start(bf16[2,1024,128]{2,1,0:T(8,128)(2,1)S(1)} %pad_maximum_fusion), channel_id=1, source_target_pairs={{0,2},{1,3},{2,4},{3,5},{4,6},{5,7},{6,8},{7,9},{8,10},{9,11},{10,... | collective-permute-start | bytes 1572872 | tf_op jit(solution)/shard_map/ppermute | solution.py:367
  18.5 0.3 collective-permute-done.5.refs_10_
  18.9 0.0 collective-permute-done.1.refs_5_
  18.9 0.0 collective-permute-done.2.refs_6_
  18.9 15.0 %attend.2 = (bf16[512,2048]{1,0:T(8,128)(2,1)}, bf16[512,2048]{1,0:T(8,128)(2,1)}, bf16[2,512,512]{2,1,0:T(8,128)(2,1)S(1)}, f32[2,1024,128]{2,1,0:T(8,128)S(1)}, bf16[2,1024,128]{2,1,0:T(8,128)(2,1)S(1)}) custom-call(s32[48]{0:T(128)S(1)} %reshape.19.refs_0_, s32[8]{0:T(128)S(1)} %copy-done, s32[1]{0:T(128)} %bitcast.1.refs_2_, bf16[512,2048]{1,0:T(8,128)(2,1)} %refs_3_.3, ...), custom_call_target="tpu_custom_call" | custom-call | flops 4026531840 | bytes 10485760 | tf_op jit(solution)/shard_map/attend/pallas_call | solution.py:229
  33.9 2.1 %collective-permute-start.9 = (bf16[2,1024,128]{2,1,0:T(8,128)(2,1)S(1)}, bf16[2,1024,128]{2,1,0:T(8,128)(2,1)S(1)}, u32[]{:S(2)}, u32[]{:S(2)}) collective-permute-start(bf16[2,1024,128]{2,1,0:T(8,128)(2,1)S(1)} %get-tuple-element.47), channel_id=1, source_target_pairs={{2,0},{3,1},{4,2},{5,3},{6,4},{7,5},{8,6},{9,7},{10,8},{11,9},{12,... | collective-permute-start | bytes 1572872 | tf_op jit(solution)/shard_map/ppermute | solution.py:367
  36.0 1.0 %collective-permute-start.6 = (bf16[2,512,512]{2,1,0:T(8,128)(2,1)S(1)}, bf16[2,512,512]{2,1,0:T(8,128)(2,1)S(1)}, u32[]{:S(2)}, u32[]{:S(2)}) collective-permute-start(bf16[2,512,512]{2,1,0:T(8,128)(2,1)S(1)} %get-tuple-element.37), channel_id=1, source_target_pairs={{0,1},{1,0},{2,3},{3,2},{4,5},{5,4},{6,7},{7,6},{8,9},{9,8},{10,11... | collective-permute-start | bytes 3145736 | tf_op jit(solution)/shard_map/ppermute | solution.py:367
  36.9 13.9 %attend.3 = (bf16[512,2048]{1,0:T(8,128)(2,1)}, bf16[512,2048]{1,0:T(8,128)(2,1)}, bf16[2,512,512]{2,1,0:T(8,128)(2,1)S(1)}, f32[2,512,128]{2,1,0:T(8,128)S(1)},...) custom-call(s32[48]{0:T(128)S(1)} %reshape.19.refs_0_, ...), custom_call_target="tpu_custom_call", output_to_operand_aliasing={{0}: (10, {}), {1}: (11, {})} | custom-call | flops 4026531840 | bytes 10485760 | tf_op jit(solution)/shard_map/attend/pallas_call | solution.py:229
  50.9 0.5 collective-permute-done.9.back
  51.4 0.0 collective-permute-start.10
  51.4 1.9 %collective-permute-start.11 = (bf16[2,512,128]{2,1,0:T(8,128)(2,1)S(1)}, bf16[2,512,128]{2,1,0:T(8,128)(2,1)S(1)}, u32[]{:S(2)}, u32[]{:S(2)}) collective-permute-start(bf16[2,512,128]{2,1,0:T(8,128)(2,1)S(1)} %get-tuple-element.53), channel_id=1, source_target_pairs={{3,0},{2,1},{5,2},{4,3},{7,4},{6,5},{9,6},{8,7},{11,8},{10,9},{13,... | collective-permute-start | bytes 786440 | tf_op jit(solution)/shard_map/ppermute | solution.py:367
  53.4 0.1 total.1
  53.5 0.5 collective-permute-start.12
  54.0 1.9 %collective-permute-start.13 = (bf16[2,512,128]{2,1,0:T(8,128)(2,1)S(1)}, bf16[2,512,128]{2,1,0:T(8,128)(2,1)S(1)}, u32[]{:S(2)}, u32[]{:S(2)}) collective-permute-start(bf16[2,512,128]{2,1,0:T(8,128)(2,1)S(1)} %get-tuple-element.61), channel_id=1, source_target_pairs={{2,0},{3,1},{4,2},{5,3},{6,4},{7,5},{8,6},{9,7},{10,8},{11,9},{12,... | collective-permute-start | bytes 786440 | tf_op jit(solution)/shard_map/ppermute | solution.py:367
  56.0 0.3 collective-permute-start.14
  56.2 2.1 %place.1 = (bf16[512,2048]{1,0:T(8,128)(2,1)}, bf16[512,2048]{1,0:T(8,128)(2,1)}) custom-call(s32[1]{0:T(128)} %bitcast.core, bf16[2,512,512]{2,1,0:T(8,128)(2,1)S(1)} %collective-permute-done.6.refs_0_, bf16[2,512,512]{2,1,0:T(8,128)(2,1)S(1)} %collective-permute-done.10.refs_1_, ...), custom_call_target="tpu_custom_call", output_to_operand_aliasing={{0}: (3, {}), {1}: (4, {})} | custom-call | tf_op jit(solution)/shard_map/place/pallas_call | solution.py:285
  58.3 3.9 %collective-permute-done.11.refs_5_ = bf16[2,512,128]{2,1,0:T(8,128)(2,1)S(1)} collective-permute-done((bf16[2,512,128]{2,1,0:T(8,128)(2,1)S(1)}, bf16[2,512,128]{2,1,0:T(8,128)(2,1)S(1)}, u32[]{:S(2)}, u32[]{:S(2)}) %collective-permute-start.11) | collective-permute-done | bytes 262176 | tf_op jit(solution)/shard_map/ppermute | solution.py:367
  62.2 6.2 %collective-permute-done.13.refs_3_ = bf16[2,512,128]{2,1,0:T(8,128)(2,1)S(1)} collective-permute-done((bf16[2,512,128]{2,1,0:T(8,128)(2,1)S(1)}, bf16[2,512,128]{2,1,0:T(8,128)(2,1)S(1)}, u32[]{:S(2)}, u32[]{:S(2)}) %collective-permute-start.13) | collective-permute-done | bytes 262176 | tf_op jit(solution)/shard_map/ppermute | solution.py:367
  68.4 1.2 %grads.1 = (bf16[512,512]{1,0:T(8,128)(2,1)}, bf16[512,512]{1,0:T(8,128)(2,1)}) custom-call(s32[1]{0:T(128)} %bitcast.core, bf16[2,512,128]{2,1,0:T(8,128)(2,1)S(1)} %get-tuple-element.58.refs_0_, bf16[2,512,128]{2,1,0:T(8,128)(2,1)S(1)} %collective-permute-done.12.refs_1_, f32[2,512,128]{2,1,0:T(8,128)S(1)} %get-tuple-element.60.refs_2_, ...), custom_call_target="tpu_custom_call" | custom-call | tf_op jit(solution)/shard_map/grads/pallas_call | solution.py:339
  (9 shorter events, 0.1 us)
Async XLA Ops:
  0.6 18.3 %copy-start = (s32[8]{0:T(128)S(1)}, s32[8]{0:T(128)}, u32[]{:S(2)}) copy-start(s32[8]{0:T(128)} %refs_1_.3) | copy-start | bytes 100
  0.6 18.2 %collective-permute-start.1 = (bf16[512,2048]{1,0:T(8,128)(2,1)}, bf16[512,2048]{1,0:T(8,128)(2,1)S(1)}, u32[]{:S(2)}, u32[]{:S(2)}) collective-permute-start(bf16[512,2048]{1,0:T(8,128)(2,1)} %refs_3_.3), channel_id=1, source_target_pairs={{0,1},{1,0},{2,3},{3,2},{4,5},{5,4},{6,7},{7,6},{8,9},{9,8},{10,11... | collective-permute-start | bytes 6291464 | tf_op jit(solution)/shard_map/ppermute | solution.py:367
  0.7 18.2 %collective-permute-start.2 = (bf16[512,2048]{1,0:T(8,128)(2,1)}, bf16[512,2048]{1,0:T(8,128)(2,1)}, u32[]{:S(2)}, u32[]{:S(2)}) collective-permute-start(bf16[512,2048]{1,0:T(8,128)(2,1)} %refs_4_.3), channel_id=1, source_target_pairs={{0,1},{1,0},{2,3},{3,2},{4,5},{5,4},{6,7},{7,6},{8,9},{9,8},{10,11... | collective-permute-start | bytes 6291464 | tf_op jit(solution)/shard_map/ppermute | solution.py:367
  2.6 7.8 %collective-permute-start.7 = (bf16[2,512,128]{2,1,0:T(8,128)(2,1)S(1)}, bf16[2,512,128]{2,1,0:T(8,128)(2,1)S(1)}, u32[]{:S(2)}, u32[]{:S(2)}) collective-permute-start(bf16[2,512,128]{2,1,0:T(8,128)(2,1)S(1)} %get-tuple-element.39), channel_id=1, source_target_pairs={{0,1},{1,0},{2,3},{3,2},{4,5},{5,4},{6,7},{7,6},{8,9},{9,8},{10,11... | collective-permute-start | bytes 786440 | tf_op jit(solution)/shard_map/ppermute | solution.py:367
  2.7 4.5 %collective-permute-start = (s32[4,6]{1,0:T(4,128)}, s32[4,6]{1,0:T(4,128)S(1)}, u32[]{:S(2)}, u32[]{:S(2)}) collective-permute-start(s32[4,6]{1,0:T(4,128)} %param.11), channel_id=1, source_target_pairs={{0,1},{1,0},{2,3},{3,2},{4,5},{5,4},{6,7},{7,6},{8,9},{9,8},{10,11... | collective-permute-start | bytes 296 | tf_op jit(solution)/shard_map/ppermute | solution.py:367
  3.2 11.0 %collective-permute-start.4 = (bf16[2,512,128]{2,1,0:T(8,128)(2,1)S(1)}, bf16[2,512,128]{2,1,0:T(8,128)(2,1)S(1)}, u32[]{:S(2)}, u32[]{:S(2)}) collective-permute-start(bf16[2,512,128]{2,1,0:T(8,128)(2,1)S(1)} %get-tuple-element.35.refs_7_), channel_id=1, source_target_pairs={{0,2},{1,3},{2,4},{3,5},{4,6},{5,7},{6,8},{7,9},{8,10},{9,11},{10,... | collective-permute-start | bytes 786440 | tf_op jit(solution)/shard_map/ppermute | solution.py:367
  7.3 11.6 %collective-permute-start.5 = (bf16[2,512,128]{2,1,0:T(8,128)(2,1)S(1)}, bf16[2,512,128]{2,1,0:T(8,128)(2,1)}, u32[]{:S(2)}, u32[]{:S(2)}) collective-permute-start(bf16[2,512,128]{2,1,0:T(8,128)(2,1)S(1)} %get-tuple-element.36), channel_id=1, source_target_pairs={{0,3},{1,2},{2,5},{3,4},{4,7},{5,6},{6,9},{7,8},{8,11},{9,10},{10,... | collective-permute-start | bytes 786440 | tf_op jit(solution)/shard_map/ppermute | solution.py:367
  10.5 8.4 %collective-permute-start.3 = (bf16[2,512,128]{2,1,0:T(8,128)(2,1)S(1)}, bf16[2,512,128]{2,1,0:T(8,128)(2,1)}, u32[]{:S(2)}, u32[]{:S(2)}) collective-permute-start(bf16[2,512,128]{2,1,0:T(8,128)(2,1)S(1)} %get-tuple-element.36), channel_id=1, source_target_pairs={{0,1},{1,0},{2,3},{3,2},{4,5},{5,4},{6,7},{7,6},{8,9},{9,8},{10,11... | collective-permute-start | bytes 786440 | tf_op jit(solution)/shard_map/ppermute | solution.py:367
  14.2 22.7 %collective-permute-start.8 = (bf16[2,1024,128]{2,1,0:T(8,128)(2,1)S(1)}, bf16[2,1024,128]{2,1,0:T(8,128)(2,1)S(1)}, u32[]{:S(2)}, u32[]{:S(2)}) collective-permute-start(bf16[2,1024,128]{2,1,0:T(8,128)(2,1)S(1)} %pad_maximum_fusion), channel_id=1, source_target_pairs={{0,2},{1,3},{2,4},{3,5},{4,6},{5,7},{6,8},{7,9},{8,10},{9,11},{10,... | collective-permute-start | bytes 1572872 | tf_op jit(solution)/shard_map/ppermute | solution.py:367
  33.9 17.5 %collective-permute-start.9 = (bf16[2,1024,128]{2,1,0:T(8,128)(2,1)S(1)}, bf16[2,1024,128]{2,1,0:T(8,128)(2,1)S(1)}, u32[]{:S(2)}, u32[]{:S(2)}) collective-permute-start(bf16[2,1024,128]{2,1,0:T(8,128)(2,1)S(1)} %get-tuple-element.47), channel_id=1, source_target_pairs={{2,0},{3,1},{4,2},{5,3},{6,4},{7,5},{8,6},{9,7},{10,8},{11,9},{12,... | collective-permute-start | bytes 1572872 | tf_op jit(solution)/shard_map/ppermute | solution.py:367
  36.0 20.0 %collective-permute-start.6 = (bf16[2,512,512]{2,1,0:T(8,128)(2,1)S(1)}, bf16[2,512,512]{2,1,0:T(8,128)(2,1)S(1)}, u32[]{:S(2)}, u32[]{:S(2)}) collective-permute-start(bf16[2,512,512]{2,1,0:T(8,128)(2,1)S(1)} %get-tuple-element.37), channel_id=1, source_target_pairs={{0,1},{1,0},{2,3},{3,2},{4,5},{5,4},{6,7},{7,6},{8,9},{9,8},{10,11... | collective-permute-start | bytes 3145736 | tf_op jit(solution)/shard_map/ppermute | solution.py:367
  51.4 4.8 %collective-permute-start.10 = (bf16[2,512,512]{2,1,0:T(8,128)(2,1)S(1)}, bf16[2,512,512]{2,1,0:T(8,128)(2,1)S(1)}, u32[]{:S(2)}, u32[]{:S(2)}) collective-permute-start(bf16[2,512,512]{2,1,0:T(8,128)(2,1)S(1)} %get-tuple-element.48), channel_id=1, source_target_pairs={{0,1},{1,0},{2,3},{3,2},{4,5},{5,4},{6,7},{7,6},{8,9},{9,8},{10,11... | collective-permute-start | bytes 3145736 | tf_op jit(solution)/shard_map/ppermute | solution.py:367
  51.4 10.8 %collective-permute-start.11 = (bf16[2,512,128]{2,1,0:T(8,128)(2,1)S(1)}, bf16[2,512,128]{2,1,0:T(8,128)(2,1)S(1)}, u32[]{:S(2)}, u32[]{:S(2)}) collective-permute-start(bf16[2,512,128]{2,1,0:T(8,128)(2,1)S(1)} %get-tuple-element.53), channel_id=1, source_target_pairs={{3,0},{2,1},{5,2},{4,3},{7,4},{6,5},{9,6},{8,7},{11,8},{10,9},{13,... | collective-permute-start | bytes 786440 | tf_op jit(solution)/shard_map/ppermute | solution.py:367
  53.5 8.8 %collective-permute-start.12 = (bf16[2,512,128]{2,1,0:T(8,128)(2,1)S(1)}, bf16[2,512,128]{2,1,0:T(8,128)(2,1)S(1)}, u32[]{:S(2)}, u32[]{:S(2)}) collective-permute-start(bf16[2,512,128]{2,1,0:T(8,128)(2,1)S(1)} %get-tuple-element.59), channel_id=1, source_target_pairs={{0,1},{1,0},{2,3},{3,2},{4,5},{5,4},{6,7},{7,6},{8,9},{9,8},{10,11... | collective-permute-start | bytes 786440 | tf_op jit(solution)/shard_map/ppermute | solution.py:367
  54.0 14.4 %collective-permute-start.13 = (bf16[2,512,128]{2,1,0:T(8,128)(2,1)S(1)}, bf16[2,512,128]{2,1,0:T(8,128)(2,1)S(1)}, u32[]{:S(2)}, u32[]{:S(2)}) collective-permute-start(bf16[2,512,128]{2,1,0:T(8,128)(2,1)S(1)} %get-tuple-element.61), channel_id=1, source_target_pairs={{2,0},{3,1},{4,2},{5,3},{6,4},{7,5},{8,6},{9,7},{10,8},{11,9},{12,... | collective-permute-start | bytes 786440 | tf_op jit(solution)/shard_map/ppermute | solution.py:367
  56.0 12.5 %collective-permute-start.14 = (bf16[2,512,128]{2,1,0:T(8,128)(2,1)S(1)}, bf16[2,512,128]{2,1,0:T(8,128)(2,1)S(1)}, u32[]{:S(2)}, u32[]{:S(2)}) collective-permute-start(bf16[2,512,128]{2,1,0:T(8,128)(2,1)S(1)} %get-tuple-element.62), channel_id=1, source_target_pairs={{0,1},{1,0},{2,3},{3,2},{4,5},{5,4},{6,7},{7,6},{8,9},{9,8},{10,11... | collective-permute-start | bytes 786440 | tf_op jit(solution)/shard_map/ppermute | solution.py:367

commit v4 on v3

--- a/solution.py
+++ b/solution.py
@@ -375,8 +375,9 @@
             prev.append([send(mine, same), send(theirs, cross)])
         else:
             prev.append([send(jnp.concatenate([mine, sib[h]], axis=1), same)])
-    sib_queries, sib_out_grad = send(queries, pairs), send(out_grad, pairs)
-    lists = jnp.concatenate([block_lists, send(block_lists, pairs)])
+    late, _ = lax.optimization_barrier(((queries, out_grad, block_lists), packed))
+    sib_queries, sib_out_grad, sib_lists = [send(value, pairs) for value in late]
+    lists = jnp.concatenate([block_lists, sib_lists])
 
     full, returned, pieces, back = (), [], [], None
     for h in range(PER_CORE):

time: 69.7 us -> 69 us (0.990)
  starting transfers between devices: 20.2 us -> 24.7 us
  Pallas kernels: 33.6 us -> 30.5 us
  waiting for transfers between devices: 14.2 us -> 11.8 us
    ppermute x15, starting transfers between devices: 20.2 us -> 24.7 us  [send(): return lax.ppermute(value, 'ctx', route)]
    pallas_call x2, Pallas kernels: 28.9 us -> 25.7 us  [attend(): pl.pallas_call(kernel, grid_spec=pltpu.PrefetchScalarGridSpec(num_scalar_...]
    ppermute x15, waiting for transfers between devices: 14.2 us -> 11.8 us  [send(): return lax.ppermute(value, 'ctx', route)]
  transfers between devices with their start and end apart: 15 -> 15, of which waited for: 6 -> 5; matrix products, arithmetic and copies ran while one was open for 1% -> 1% of each run, Pallas kernels for 47% -> 41%
where the time goes in v4:
time: 69 us; the launch traced here: 68.6 us
  Pallas kernels  30.5 us (44%)
  starting transfers between devices  24.7 us (36%)
  waiting for transfers between devices  11.8 us (17%)
  between operations  0.78 us (1%)
  other arithmetic  0.72 us (1%)
    pallas_call x2, Pallas kernels, attend(): pl.pallas_call(kernel, grid_spec=pltpu.PrefetchScalarGridSpec(num_scalar_...  25.7 us
    ppermute x15, starting transfers between devices, send(): return lax.ppermute(value, 'ctx', route)  24.7 us
    ppermute x15, waiting for transfers between devices, send(): return lax.ppermute(value, 'ctx', route)  11.8 us
    pallas_call x1, Pallas kernels, place(): pl.pallas_call(place_kernel, grid_spec=pltpu.PrefetchScalarGridSpec(num_s...  2.1 us
    pallas_call x1, Pallas kernels, pack(): pl.pallas_call(pack_kernel, grid_spec=pltpu.PrefetchScalarGridSpec(num_sc...  1.38 us
  transfers between devices with their start and end apart: 15, of which 5 were waited for; matrix products, arithmetic and copies ran while one was open for 1% of the time, Pallas kernels for 41%

profile of v4, /device:TPU:22, one launch (start us, length us, event | category | flops | bytes accessed | tf_op | source)
XLA Modules:
  0.0 68.6 jit_solution(11837246852482796513)
XLA Ops:
  0.6 1.4 %pack.1 = (bf16[2,512,128]{2,1,0:T(8,128)(2,1)S(1)}, bf16[2,512,128]{2,1,0:T(8,128)(2,1)S(1)}, bf16[2,512,128]{2,1,0:T(8,128)(2,1)S(1)}, bf16[2,512,128]{2,1,0:T(8,128)(2,1)S(1)}) custom-call(s32[1]{0:T(128)} %bitcast.core, bf16[512,512]{1,0:T(8,128)(2,1)} %keys.1, bf16[512,512]{1,0:T(8,128)(2,1)} %values.1), custom_call_target="tpu_custom_call" | custom-call | tf_op jit(solution)/shard_map/pack/pallas_call | solution.py:50
  2.0 0.1 collective-permute-start.1
  2.1 0.5 collective-permute-start.2
  2.6 0.1 collective-permute-start.7
  2.7 0.4 collective-permute-start
  3.1 3.4 %collective-permute-start.4 = (bf16[2,512,128]{2,1,0:T(8,128)(2,1)S(1)}, bf16[2,512,128]{2,1,0:T(8,128)(2,1)S(1)}, u32[]{:S(2)}, u32[]{:S(2)}) collective-permute-start(bf16[2,512,128]{2,1,0:T(8,128)(2,1)S(1)} %get-tuple-element.38.refs_7_), channel_id=1, source_target_pairs={{0,2},{1,3},{2,4},{3,5},{4,6},{5,7},{6,8},{7,9},{8,10},{9,11},{10,... | collective-permute-start | bytes 786440 | tf_op jit(solution)/shard_map/ppermute | solution.py:367
  6.5 2.1 %collective-permute-done = s32[4,6]{1,0:T(4,128)S(1)} collective-permute-done((s32[4,6]{1,0:T(4,128)}, s32[4,6]{1,0:T(4,128)S(1)}, u32[]{:S(2)}, u32[]{:S(2)}) %collective-permute-start) | collective-permute-done | bytes 128 | tf_op jit(solution)/shard_map/ppermute | solution.py:367
  8.7 3.2 %collective-permute-start.5 = (bf16[2,512,128]{2,1,0:T(8,128)(2,1)S(1)}, bf16[2,512,128]{2,1,0:T(8,128)(2,1)}, u32[]{:S(2)}, u32[]{:S(2)}) collective-permute-start(bf16[2,512,128]{2,1,0:T(8,128)(2,1)S(1)} %get-tuple-element.39), channel_id=1, source_target_pairs={{0,3},{1,2},{2,5},{3,4},{4,7},{5,6},{6,9},{7,8},{8,11},{9,10},{10,... | collective-permute-start | bytes 786440 | tf_op jit(solution)/shard_map/ppermute | solution.py:367
  11.8 0.0 collective-permute-done.7.refs_8_
  11.8 0.4 collective-permute-start.3
  12.3 0.7 %pad_add_fusion = s32[8,6]{1,0:T(8,128)S(1)} fusion(s32[4,6]{1,0:T(4,128)S(1)} %collective-permute-done, s32[4,6]{1,0:T(4,128)} %param.11), kind=kLoop, calls=%fused_computation.1 | loop fusion | flops 48 | bytes 384 | tf_op jit(solution)/shard_map/concatenate | solution.py:380
  13.0 0.1 reshape.19.refs_0_
  13.1 0.2 collective-permute-done.4.refs_9_
  13.3 4.3 %collective-permute-start.8 = (bf16[2,1024,128]{2,1,0:T(8,128)(2,1)S(1)}, bf16[2,1024,128]{2,1,0:T(8,128)(2,1)S(1)}, u32[]{:S(2)}, u32[]{:S(2)}) collective-permute-start(bf16[2,1024,128]{2,1,0:T(8,128)(2,1)S(1)} %pad_maximum_fusion), channel_id=1, source_target_pairs={{0,2},{1,3},{2,4},{3,5},{4,6},{5,7},{6,8},{7,9},{8,10},{9,11},{10,... | collective-permute-start | bytes 1572872 | tf_op jit(solution)/shard_map/ppermute | solution.py:367
  17.6 1.3 %collective-permute-done.5.refs_10_ = bf16[2,512,128]{2,1,0:T(8,128)(2,1)} collective-permute-done((bf16[2,512,128]{2,1,0:T(8,128)(2,1)S(1)}, bf16[2,512,128]{2,1,0:T(8,128)(2,1)}, u32[]{:S(2)}, u32[]{:S(2)}) %collective-permute-start.5) | collective-permute-done | bytes 262176 | tf_op jit(solution)/shard_map/ppermute | solution.py:367
  18.9 0.0 collective-permute-done.3.refs_8_
  18.9 0.0 collective-permute-done.1.refs_5_
  18.9 0.0 collective-permute-done.2.refs_6_
  19.0 13.4 %attend.2 = (bf16[512,2048]{1,0:T(8,128)(2,1)}, bf16[512,2048]{1,0:T(8,128)(2,1)}, bf16[2,512,512]{2,1,0:T(8,128)(2,1)S(1)}, f32[2,1024,128]{2,1,0:T(8,128)S(1)}, bf16[2,1024,128]{2,1,0:T(8,128)(2,1)S(1)}) custom-call(s32[48]{0:T(128)S(1)} %reshape.19.refs_0_, s32[8]{0:T(128)S(1)} %copy-done, s32[1]{0:T(128)} %bitcast.1.refs_2_, bf16[512,2048]{1,0:T(8,128)(2,1)} %refs_3_.3, ...), custom_call_target="tpu_custom_call" | custom-call | flops 4026531840 | bytes 10485760 | tf_op jit(solution)/shard_map/attend/pallas_call | solution.py:229
  32.4 5.1 %collective-permute-start.9 = (bf16[2,1024,128]{2,1,0:T(8,128)(2,1)S(1)}, bf16[2,1024,128]{2,1,0:T(8,128)(2,1)S(1)}, u32[]{:S(2)}, u32[]{:S(2)}) collective-permute-start(bf16[2,1024,128]{2,1,0:T(8,128)(2,1)S(1)} %get-tuple-element.53), channel_id=1, source_target_pairs={{2,0},{3,1},{4,2},{5,3},{6,4},{7,5},{8,6},{9,7},{10,8},{11,9},{12,... | collective-permute-start | bytes 1572872 | tf_op jit(solution)/shard_map/ppermute | solution.py:367
  37.5 0.2 collective-permute-start.6
  37.7 12.3 %attend.3 = (bf16[512,2048]{1,0:T(8,128)(2,1)}, bf16[512,2048]{1,0:T(8,128)(2,1)}, bf16[2,512,512]{2,1,0:T(8,128)(2,1)S(1)}, f32[2,512,128]{2,1,0:T(8,128)S(1)},...) custom-call(s32[48]{0:T(128)S(1)} %reshape.19.refs_0_, ...), custom_call_target="tpu_custom_call", output_to_operand_aliasing={{0}: (10, {}), {1}: (11, {})} | custom-call | flops 4026531840 | bytes 10485760 | tf_op jit(solution)/shard_map/attend/pallas_call | solution.py:229
  50.0 0.4 collective-permute-start.10
  50.4 3.7 %collective-permute-start.11 = (bf16[2,512,128]{2,1,0:T(8,128)(2,1)S(1)}, bf16[2,512,128]{2,1,0:T(8,128)(2,1)S(1)}, u32[]{:S(2)}, u32[]{:S(2)}) collective-permute-start(bf16[2,512,128]{2,1,0:T(8,128)(2,1)S(1)} %get-tuple-element.59), channel_id=1, source_target_pairs={{3,0},{2,1},{5,2},{4,3},{7,4},{6,5},{9,6},{8,7},{11,8},{10,9},{13,... | collective-permute-start | bytes 786440 | tf_op jit(solution)/shard_map/ppermute | solution.py:367
  54.1 0.1 total.1
  54.2 0.1 collective-permute-start.12
  54.4 2.5 %collective-permute-start.13 = (bf16[2,512,128]{2,1,0:T(8,128)(2,1)S(1)}, bf16[2,512,128]{2,1,0:T(8,128)(2,1)S(1)}, u32[]{:S(2)}, u32[]{:S(2)}) collective-permute-start(bf16[2,512,128]{2,1,0:T(8,128)(2,1)S(1)} %get-tuple-element.67), channel_id=1, source_target_pairs={{2,0},{3,1},{4,2},{5,3},{6,4},{7,5},{8,6},{9,7},{10,8},{11,9},{12,... | collective-permute-start | bytes 786440 | tf_op jit(solution)/shard_map/ppermute | solution.py:367
  56.9 0.3 collective-permute-start.14
  57.1 2.1 %place.1 = (bf16[512,2048]{1,0:T(8,128)(2,1)}, bf16[512,2048]{1,0:T(8,128)(2,1)}) custom-call(s32[1]{0:T(128)} %bitcast.core, bf16[2,512,512]{2,1,0:T(8,128)(2,1)S(1)} %collective-permute-done.6.refs_0_, bf16[2,512,512]{2,1,0:T(8,128)(2,1)S(1)} %collective-permute-done.10.refs_1_, ...), custom_call_target="tpu_custom_call", output_to_operand_aliasing={{0}: (3, {}), {1}: (4, {})} | custom-call | tf_op jit(solution)/shard_map/place/pallas_call | solution.py:285
  59.2 2.3 %collective-permute-done.11.refs_5_ = bf16[2,512,128]{2,1,0:T(8,128)(2,1)S(1)} collective-permute-done((bf16[2,512,128]{2,1,0:T(8,128)(2,1)S(1)}, bf16[2,512,128]{2,1,0:T(8,128)(2,1)S(1)}, u32[]{:S(2)}, u32[]{:S(2)}) %collective-permute-start.11) | collective-permute-done | bytes 262176 | tf_op jit(solution)/shard_map/ppermute | solution.py:367
  61.5 5.9 %collective-permute-done.13.refs_3_ = bf16[2,512,128]{2,1,0:T(8,128)(2,1)S(1)} collective-permute-done((bf16[2,512,128]{2,1,0:T(8,128)(2,1)S(1)}, bf16[2,512,128]{2,1,0:T(8,128)(2,1)S(1)}, u32[]{:S(2)}, u32[]{:S(2)}) %collective-permute-start.13) | collective-permute-done | bytes 262176 | tf_op jit(solution)/shard_map/ppermute | solution.py:367
  67.4 1.2 %grads.1 = (bf16[512,512]{1,0:T(8,128)(2,1)}, bf16[512,512]{1,0:T(8,128)(2,1)}) custom-call(s32[1]{0:T(128)} %bitcast.core, bf16[2,512,128]{2,1,0:T(8,128)(2,1)S(1)} %get-tuple-element.64.refs_0_, bf16[2,512,128]{2,1,0:T(8,128)(2,1)S(1)} %collective-permute-done.12.refs_1_, f32[2,512,128]{2,1,0:T(8,128)S(1)} %get-tuple-element.66.refs_2_, ...), custom_call_target="tpu_custom_call" | custom-call | tf_op jit(solution)/shard_map/grads/pallas_call | solution.py:339
  (9 shorter events, 0.1 us)
Async XLA Ops:
  0.6 18.3 %copy-start = (s32[8]{0:T(128)S(1)}, s32[8]{0:T(128)}, u32[]{:S(2)}) copy-start(s32[8]{0:T(128)} %refs_1_.3) | copy-start | bytes 100
  2.0 16.9 %collective-permute-start.1 = (bf16[512,2048]{1,0:T(8,128)(2,1)}, bf16[512,2048]{1,0:T(8,128)(2,1)S(1)}, u32[]{:S(2)}, u32[]{:S(2)}) collective-permute-start(bf16[512,2048]{1,0:T(8,128)(2,1)} %refs_3_.3), channel_id=1, source_target_pairs={{0,1},{1,0},{2,3},{3,2},{4,5},{5,4},{6,7},{7,6},{8,9},{9,8},{10,11... | collective-permute-start | bytes 6291464 | tf_op jit(solution)/shard_map/ppermute | solution.py:367
  2.1 16.8 %collective-permute-start.2 = (bf16[512,2048]{1,0:T(8,128)(2,1)}, bf16[512,2048]{1,0:T(8,128)(2,1)}, u32[]{:S(2)}, u32[]{:S(2)}) collective-permute-start(bf16[512,2048]{1,0:T(8,128)(2,1)} %refs_4_.3), channel_id=1, source_target_pairs={{0,1},{1,0},{2,3},{3,2},{4,5},{5,4},{6,7},{7,6},{8,9},{9,8},{10,11... | collective-permute-start | bytes 6291464 | tf_op jit(solution)/shard_map/ppermute | solution.py:367
  2.6 9.2 %collective-permute-start.7 = (bf16[2,512,128]{2,1,0:T(8,128)(2,1)S(1)}, bf16[2,512,128]{2,1,0:T(8,128)(2,1)S(1)}, u32[]{:S(2)}, u32[]{:S(2)}) collective-permute-start(bf16[2,512,128]{2,1,0:T(8,128)(2,1)S(1)} %get-tuple-element.41), channel_id=1, source_target_pairs={{0,1},{1,0},{2,3},{3,2},{4,5},{5,4},{6,7},{7,6},{8,9},{9,8},{10,11... | collective-permute-start | bytes 786440 | tf_op jit(solution)/shard_map/ppermute | solution.py:367
  2.7 6.0 %collective-permute-start = (s32[4,6]{1,0:T(4,128)}, s32[4,6]{1,0:T(4,128)S(1)}, u32[]{:S(2)}, u32[]{:S(2)}) collective-permute-start(s32[4,6]{1,0:T(4,128)} %param.11), channel_id=1, source_target_pairs={{0,1},{1,0},{2,3},{3,2},{4,5},{5,4},{6,7},{7,6},{8,9},{9,8},{10,11... | collective-permute-start | bytes 296 | tf_op jit(solution)/shard_map/ppermute | solution.py:367
  3.1 10.2 %collective-permute-start.4 = (bf16[2,512,128]{2,1,0:T(8,128)(2,1)S(1)}, bf16[2,512,128]{2,1,0:T(8,128)(2,1)S(1)}, u32[]{:S(2)}, u32[]{:S(2)}) collective-permute-start(bf16[2,512,128]{2,1,0:T(8,128)(2,1)S(1)} %get-tuple-element.38.refs_7_), channel_id=1, source_target_pairs={{0,2},{1,3},{2,4},{3,5},{4,6},{5,7},{6,8},{7,9},{8,10},{9,11},{10,... | collective-permute-start | bytes 786440 | tf_op jit(solution)/shard_map/ppermute | solution.py:367
  8.7 10.3 %collective-permute-start.5 = (bf16[2,512,128]{2,1,0:T(8,128)(2,1)S(1)}, bf16[2,512,128]{2,1,0:T(8,128)(2,1)}, u32[]{:S(2)}, u32[]{:S(2)}) collective-permute-start(bf16[2,512,128]{2,1,0:T(8,128)(2,1)S(1)} %get-tuple-element.39), channel_id=1, source_target_pairs={{0,3},{1,2},{2,5},{3,4},{4,7},{5,6},{6,9},{7,8},{8,11},{9,10},{10,... | collective-permute-start | bytes 786440 | tf_op jit(solution)/shard_map/ppermute | solution.py:367
  11.8 7.1 %collective-permute-start.3 = (bf16[2,512,128]{2,1,0:T(8,128)(2,1)S(1)}, bf16[2,512,128]{2,1,0:T(8,128)(2,1)}, u32[]{:S(2)}, u32[]{:S(2)}) collective-permute-start(bf16[2,512,128]{2,1,0:T(8,128)(2,1)S(1)} %get-tuple-element.39), channel_id=1, source_target_pairs={{0,1},{1,0},{2,3},{3,2},{4,5},{5,4},{6,7},{7,6},{8,9},{9,8},{10,11... | collective-permute-start | bytes 786440 | tf_op jit(solution)/shard_map/ppermute | solution.py:367
  13.3 24.4 %collective-permute-start.8 = (bf16[2,1024,128]{2,1,0:T(8,128)(2,1)S(1)}, bf16[2,1024,128]{2,1,0:T(8,128)(2,1)S(1)}, u32[]{:S(2)}, u32[]{:S(2)}) collective-permute-start(bf16[2,1024,128]{2,1,0:T(8,128)(2,1)S(1)} %pad_maximum_fusion), channel_id=1, source_target_pairs={{0,2},{1,3},{2,4},{3,5},{4,6},{5,7},{6,8},{7,9},{8,10},{9,11},{10,... | collective-permute-start | bytes 1572872 | tf_op jit(solution)/shard_map/ppermute | solution.py:367
  32.4 17.7 %collective-permute-start.9 = (bf16[2,1024,128]{2,1,0:T(8,128)(2,1)S(1)}, bf16[2,1024,128]{2,1,0:T(8,128)(2,1)S(1)}, u32[]{:S(2)}, u32[]{:S(2)}) collective-permute-start(bf16[2,1024,128]{2,1,0:T(8,128)(2,1)S(1)} %get-tuple-element.53), channel_id=1, source_target_pairs={{2,0},{3,1},{4,2},{5,3},{6,4},{7,5},{8,6},{9,7},{10,8},{11,9},{12,... | collective-permute-start | bytes 1572872 | tf_op jit(solution)/shard_map/ppermute | solution.py:367
  37.5 19.4 %collective-permute-start.6 = (bf16[2,512,512]{2,1,0:T(8,128)(2,1)S(1)}, bf16[2,512,512]{2,1,0:T(8,128)(2,1)S(1)}, u32[]{:S(2)}, u32[]{:S(2)}) collective-permute-start(bf16[2,512,512]{2,1,0:T(8,128)(2,1)S(1)} %get-tuple-element.45), channel_id=1, source_target_pairs={{0,1},{1,0},{2,3},{3,2},{4,5},{5,4},{6,7},{7,6},{8,9},{9,8},{10,11... | collective-permute-start | bytes 3145736 | tf_op jit(solution)/shard_map/ppermute | solution.py:367
  50.0 7.1 %collective-permute-start.10 = (bf16[2,512,512]{2,1,0:T(8,128)(2,1)S(1)}, bf16[2,512,512]{2,1,0:T(8,128)(2,1)S(1)}, u32[]{:S(2)}, u32[]{:S(2)}) collective-permute-start(bf16[2,512,512]{2,1,0:T(8,128)(2,1)S(1)} %get-tuple-element.54), channel_id=1, source_target_pairs={{0,1},{1,0},{2,3},{3,2},{4,5},{5,4},{6,7},{7,6},{8,9},{9,8},{10,11... | collective-permute-start | bytes 3145736 | tf_op jit(solution)/shard_map/ppermute | solution.py:367
  50.4 11.1 %collective-permute-start.11 = (bf16[2,512,128]{2,1,0:T(8,128)(2,1)S(1)}, bf16[2,512,128]{2,1,0:T(8,128)(2,1)S(1)}, u32[]{:S(2)}, u32[]{:S(2)}) collective-permute-start(bf16[2,512,128]{2,1,0:T(8,128)(2,1)S(1)} %get-tuple-element.59), channel_id=1, source_target_pairs={{3,0},{2,1},{5,2},{4,3},{7,4},{6,5},{9,6},{8,7},{11,8},{10,9},{13,... | collective-permute-start | bytes 786440 | tf_op jit(solution)/shard_map/ppermute | solution.py:367
  54.2 7.3 %collective-permute-start.12 = (bf16[2,512,128]{2,1,0:T(8,128)(2,1)S(1)}, bf16[2,512,128]{2,1,0:T(8,128)(2,1)S(1)}, u32[]{:S(2)}, u32[]{:S(2)}) collective-permute-start(bf16[2,512,128]{2,1,0:T(8,128)(2,1)S(1)} %get-tuple-element.65), channel_id=1, source_target_pairs={{0,1},{1,0},{2,3},{3,2},{4,5},{5,4},{6,7},{7,6},{8,9},{9,8},{10,11... | collective-permute-start | bytes 786440 | tf_op jit(solution)/shard_map/ppermute | solution.py:367
  54.4 13.1 %collective-permute-start.13 = (bf16[2,512,128]{2,1,0:T(8,128)(2,1)S(1)}, bf16[2,512,128]{2,1,0:T(8,128)(2,1)S(1)}, u32[]{:S(2)}, u32[]{:S(2)}) collective-permute-start(bf16[2,512,128]{2,1,0:T(8,128)(2,1)S(1)} %get-tuple-element.67), channel_id=1, source_target_pairs={{2,0},{3,1},{4,2},{5,3},{6,4},{7,5},{8,6},{9,7},{10,8},{11,9},{12,... | collective-permute-start | bytes 786440 | tf_op jit(solution)/shard_map/ppermute | solution.py:367
  56.9 10.6 %collective-permute-start.14 = (bf16[2,512,128]{2,1,0:T(8,128)(2,1)S(1)}, bf16[2,512,128]{2,1,0:T(8,128)(2,1)S(1)}, u32[]{:S(2)}, u32[]{:S(2)}) collective-permute-start(bf16[2,512,128]{2,1,0:T(8,128)(2,1)S(1)} %get-tuple-element.68), channel_id=1, source_target_pairs={{0,1},{1,0},{2,3},{3,2},{4,5},{5,4},{6,7},{7,6},{8,9},{9,8},{10,11... | collective-permute-start | bytes 786440 | tf_op jit(solution)/shard_map/ppermute | solution.py:367

commit v5 on v4

--- a/solution.py
+++ b/solution.py
@@ -315,29 +315,21 @@
     )(chip_part, back)
 
 
-def grads_kernel(core, *refs):
+def early_kernel(core, *refs):
     outs = refs[-2:]
-    pieces = refs[:-2]
-    own_part, own_back, other_part, other_back = pieces[-4:]
-    for kind, scale in enumerate((SCALING, 1.0)):
+    for h in range(PER_CORE - 1):
         for which, owner in enumerate((core[0], 1 - core[0])):
-            for h in range(PER_CORE - 1):
-                at = columns(owner * PER_CORE + h, HD)
-                outs[kind][:, at] = pieces[CORES * h + which][kind]
-        at = columns(core[0] * PER_CORE + PER_CORE - 1, HD)
-        value = own_part[kind] * scale + own_back[kind].astype(F32)
-        outs[kind][:, at] = value.astype(BF16)
-        at = columns((1 - core[0]) * PER_CORE + PER_CORE - 1, HD)
-        value = other_part[kind].astype(F32) + other_back[kind].astype(F32)
-        outs[kind][:, at] = value.astype(BF16)
-
-
-def grads(core, pieces):
+            at = columns(owner * PER_CORE + h, HD)
+            for kind in range(2):
+                outs[kind][:, at] = refs[CORES * h + which][kind]
+
+
+def early_grads(core, pieces):
     rows = pieces[0].shape[1]
     strip = pl.BlockSpec((2, rows, HD), lambda i, *_: (0, 0, 0))
     out = pl.BlockSpec((rows, KV_HEADS * HD), lambda i, *_: (0, 0))
     return pl.pallas_call(
-        grads_kernel,
+        early_kernel,
         grid_spec=pltpu.PrefetchScalarGridSpec(
             num_scalar_prefetch=1,
             grid=(1,),
@@ -346,8 +338,48 @@
         ),
         out_shape=[jax.ShapeDtypeStruct((rows, KV_HEADS * HD), BF16)] * 2,
         compiler_params=SMALL,
-        name="grads",
+        name="early_grads",
     )(core, *pieces)
+
+
+def last_kernel(core, own_part, own_back, other_part, other_back, before_k, before_v, *outs):
+    step = pl.program_id(0)
+
+    @pl.when(step == 0)
+    def _():
+        for kind, scale in enumerate((SCALING, 1.0)):
+            value = own_part[kind] * scale + own_back[kind].astype(F32)
+            outs[kind][...] = value.astype(BF16)
+
+    @pl.when(step == 1)
+    def _():
+        for kind in range(2):
+            value = other_part[kind].astype(F32) + other_back[kind].astype(F32)
+            outs[kind][...] = value.astype(BF16)
+
+
+def last_grads(core, pieces, early):
+    rows = pieces[0].shape[1]
+    strip = pl.BlockSpec((2, rows, HD), lambda i, *_: (0, 0, 0))
+
+    def place_of(step, core):
+        owner = core[0] + step * (1 - 2 * core[0])
+        return 0, owner * PER_CORE + PER_CORE - 1
+
+    out = pl.BlockSpec((rows, HD), place_of)
+    return pl.pallas_call(
+        last_kernel,
+        grid_spec=pltpu.PrefetchScalarGridSpec(
+            num_scalar_prefetch=1,
+            grid=(CORES,),
+            in_specs=[strip] * len(pieces) + [ANY] * 2,
+            out_specs=[out, out],
+        ),
+        out_shape=[jax.ShapeDtypeStruct(e.shape, e.dtype) for e in early],
+        input_output_aliases={1 + len(pieces) + i: i for i in range(2)},
+        compiler_params=SMALL,
+        name="last_grads",
+    )(core, *pieces, *early)
 
 
 def per_device(queries, keys, values, out_grad, doc_starts, block_lists):
@@ -399,9 +431,12 @@
             own_back, other_back = send(to_same, same_back), send(to_cross, cross_back)
             other_part = send(sib_part, pairs)
     attended, grad_query = place(core, returned, full)
-    attended, grad_query, other_back = lax.optimization_barrier((attended, grad_query, other_back))
-    pieces += [own_part, own_back, other_part, other_back]
-    return attended, grad_query, *grads(core, pieces)
+    early = early_grads(core, pieces)
+    attended, grad_query, early, other_back = lax.optimization_barrier(
+        (attended, grad_query, early, other_back)
+    )
+    last_pieces = (own_part, own_back, other_part, other_back)
+    return attended, grad_query, *last_grads(core, last_pieces, early)
 
 
 def solution(mesh):

time: 69 us -> 69.3 us (level)
  the two profiles are of different devices: /device:TPU:22 before, /device:TPU:5 now
where the time goes in v5:
time: 69.3 us; the launch traced here: 68.9 us
  Pallas kernels  32.8 us (47%)
  starting transfers between devices  18.9 us (27%)
  waiting for transfers between devices  15.6 us (23%)
  between operations  0.78 us (1%)
  other arithmetic  0.72 us (1%)
    pallas_call x2, Pallas kernels, attend(): pl.pallas_call(kernel, grid_spec=pltpu.PrefetchScalarGridSpec(num_scalar_...  27.3 us
    ppermute x15, starting transfers between devices, send(): return lax.ppermute(value, 'ctx', route)  18.9 us
    ppermute x15, waiting for transfers between devices, send(): return lax.ppermute(value, 'ctx', route)  15.6 us
    pallas_call x1, Pallas kernels, place(): pl.pallas_call(place_kernel, grid_spec=pltpu.PrefetchScalarGridSpec(num_s...  2.12 us
  transfers between devices with their start and end apart: 15, of which 5 were waited for; matrix products, arithmetic and copies ran while one was open for 1% of the time, Pallas kernels for 44%

profile of v5, /device:TPU:5, one launch (start us, length us, event | category | flops | bytes accessed | tf_op | source)
XLA Modules:
  0.0 68.9 jit_solution(1563456875839999443)
XLA Ops:
  0.6 1.4 %pack.1 = (bf16[2,512,128]{2,1,0:T(8,128)(2,1)S(1)}, bf16[2,512,128]{2,1,0:T(8,128)(2,1)S(1)}, bf16[2,512,128]{2,1,0:T(8,128)(2,1)S(1)}, bf16[2,512,128]{2,1,0:T(8,128)(2,1)S(1)}) custom-call(s32[1]{0:T(128)} %bitcast.core, bf16[512,512]{1,0:T(8,128)(2,1)} %keys.1, bf16[512,512]{1,0:T(8,128)(2,1)} %values.1), custom_call_target="tpu_custom_call" | custom-call | tf_op jit(solution)/shard_map/pack/pallas_call | solution.py:50
  2.0 0.7 %collective-permute-start.1 = (bf16[512,2048]{1,0:T(8,128)(2,1)}, bf16[512,2048]{1,0:T(8,128)(2,1)S(1)}, u32[]{:S(2)}, u32[]{:S(2)}) collective-permute-start(bf16[512,2048]{1,0:T(8,128)(2,1)} %refs_3_.3), channel_id=1, source_target_pairs={{0,1},{1,0},{2,3},{3,2},{4,5},{5,4},{6,7},{7,6},{8,9},{9,8},{10,11... | collective-permute-start | bytes 6291464 | tf_op jit(solution)/shard_map/ppermute | solution.py:399
  2.8 0.1 collective-permute-start.2
  2.9 0.4 collective-permute-start.7
  3.3 0.1 collective-permute-start
  3.4 3.1 %collective-permute-start.4 = (bf16[2,512,128]{2,1,0:T(8,128)(2,1)S(1)}, bf16[2,512,128]{2,1,0:T(8,128)(2,1)S(1)}, u32[]{:S(2)}, u32[]{:S(2)}) collective-permute-start(bf16[2,512,128]{2,1,0:T(8,128)(2,1)S(1)} %get-tuple-element.42.refs_7_), channel_id=1, source_target_pairs={{0,2},{1,3},{2,4},{3,5},{4,6},{5,7},{6,8},{7,9},{8,10},{9,11},{10,... | collective-permute-start | bytes 786440 | tf_op jit(solution)/shard_map/ppermute | solution.py:399
  6.5 2.5 %collective-permute-done = s32[4,6]{1,0:T(4,128)S(1)} collective-permute-done((s32[4,6]{1,0:T(4,128)}, s32[4,6]{1,0:T(4,128)S(1)}, u32[]{:S(2)}, u32[]{:S(2)}) %collective-permute-start) | collective-permute-done | bytes 128 | tf_op jit(solution)/shard_map/ppermute | solution.py:399
  9.0 3.4 %collective-permute-start.5 = (bf16[2,512,128]{2,1,0:T(8,128)(2,1)S(1)}, bf16[2,512,128]{2,1,0:T(8,128)(2,1)}, u32[]{:S(2)}, u32[]{:S(2)}) collective-permute-start(bf16[2,512,128]{2,1,0:T(8,128)(2,1)S(1)} %get-tuple-element.43), channel_id=1, source_target_pairs={{0,3},{1,2},{2,5},{3,4},{4,7},{5,6},{6,9},{7,8},{8,11},{9,10},{10,... | collective-permute-start | bytes 786440 | tf_op jit(solution)/shard_map/ppermute | solution.py:399
  12.4 0.0 collective-permute-done.7.refs_8_
  12.4 0.2 collective-permute-start.3
  12.6 0.7 %pad_add_fusion = s32[8,6]{1,0:T(8,128)S(1)} fusion(s32[4,6]{1,0:T(4,128)S(1)} %collective-permute-done, s32[4,6]{1,0:T(4,128)} %param.11), kind=kLoop, calls=%fused_computation.1 | loop fusion | flops 48 | bytes 384 | tf_op jit(solution)/shard_map/concatenate | solution.py:412
  13.3 0.1 reshape.19.refs_0_
  13.4 3.3 %collective-permute-start.8 = (bf16[2,1024,128]{2,1,0:T(8,128)(2,1)S(1)}, bf16[2,1024,128]{2,1,0:T(8,128)(2,1)S(1)}, u32[]{:S(2)}, u32[]{:S(2)}) collective-permute-start(bf16[2,1024,128]{2,1,0:T(8,128)(2,1)S(1)} %pad_maximum_fusion), channel_id=1, source_target_pairs={{0,2},{1,3},{2,4},{3,5},{4,6},{5,7},{6,8},{7,9},{8,10},{9,11},{10,... | collective-permute-start | bytes 1572872 | tf_op jit(solution)/shard_map/ppermute | solution.py:399
  16.7 2.8 %collective-permute-done.5.refs_10_ = bf16[2,512,128]{2,1,0:T(8,128)(2,1)} collective-permute-done((bf16[2,512,128]{2,1,0:T(8,128)(2,1)S(1)}, bf16[2,512,128]{2,1,0:T(8,128)(2,1)}, u32[]{:S(2)}, u32[]{:S(2)}) %collective-permute-start.5) | collective-permute-done | bytes 262176 | tf_op jit(solution)/shard_map/ppermute | solution.py:399
  19.6 0.0 collective-permute-done.3.refs_8_
  19.6 0.0 collective-permute-done.1.refs_5_
  19.6 14.2 %attend.2 = (bf16[512,2048]{1,0:T(8,128)(2,1)}, bf16[512,2048]{1,0:T(8,128)(2,1)}, bf16[2,512,512]{2,1,0:T(8,128)(2,1)S(1)}, f32[2,1024,128]{2,1,0:T(8,128)S(1)}, bf16[2,1024,128]{2,1,0:T(8,128)(2,1)S(1)}) custom-call(s32[48]{0:T(128)S(1)} %reshape.19.refs_0_, s32[8]{0:T(128)S(1)} %copy-done, s32[1]{0:T(128)} %bitcast.1.refs_2_, bf16[512,2048]{1,0:T(8,128)(2,1)} %refs_3_.3, ...), custom_call_target="tpu_custom_call" | custom-call | flops 4026531840 | bytes 10485760 | tf_op jit(solution)/shard_map/attend/pallas_call | solution.py:229
  33.8 2.1 %collective-permute-start.9 = (bf16[2,1024,128]{2,1,0:T(8,128)(2,1)S(1)}, bf16[2,1024,128]{2,1,0:T(8,128)(2,1)S(1)}, u32[]{:S(2)}, u32[]{:S(2)}) collective-permute-start(bf16[2,1024,128]{2,1,0:T(8,128)(2,1)S(1)} %get-tuple-element.57), channel_id=1, source_target_pairs={{2,0},{3,1},{4,2},{5,3},{6,4},{7,5},{8,6},{9,7},{10,8},{11,9},{12,... | collective-permute-start | bytes 1572872 | tf_op jit(solution)/shard_map/ppermute | solution.py:399
  35.9 0.1 collective-permute-start.6
  36.0 13.1 %attend.3 = (bf16[512,2048]{1,0:T(8,128)(2,1)}, bf16[512,2048]{1,0:T(8,128)(2,1)}, bf16[2,512,512]{2,1,0:T(8,128)(2,1)S(1)}, f32[2,512,128]{2,1,0:T(8,128)S(1)},...) custom-call(s32[48]{0:T(128)S(1)} %reshape.19.refs_0_, ...), custom_call_target="tpu_custom_call", output_to_operand_aliasing={{0}: (10, {}), {1}: (11, {})} | custom-call | flops 4026531840 | bytes 10485760 | tf_op jit(solution)/shard_map/attend/pallas_call | solution.py:229
  49.1 1.0 %collective-permute-done.9.back = bf16[2,1024,128]{2,1,0:T(8,128)(2,1)S(1)} collective-permute-done((bf16[2,1024,128]{2,1,0:T(8,128)(2,1)S(1)}, bf16[2,1024,128]{2,1,0:T(8,128)(2,1)S(1)}, u32[]{:S(2)}, u32[]{:S(2)}) %collective-permute-start.9) | collective-permute-done | bytes 524320 | tf_op jit(solution)/shard_map/ppermute | solution.py:399
  50.1 0.8 %collective-permute-start.10 = (bf16[2,512,512]{2,1,0:T(8,128)(2,1)S(1)}, bf16[2,512,512]{2,1,0:T(8,128)(2,1)S(1)}, u32[]{:S(2)}, u32[]{:S(2)}) collective-permute-start(bf16[2,512,512]{2,1,0:T(8,128)(2,1)S(1)} %get-tuple-element.58), channel_id=1, source_target_pairs={{0,1},{1,0},{2,3},{3,2},{4,5},{5,4},{6,7},{7,6},{8,9},{9,8},{10,11... | collective-permute-start | bytes 3145736 | tf_op jit(solution)/shard_map/ppermute | solution.py:399
  50.9 0.1 total.1
  51.0 0.1 collective-permute-start.11
  51.1 1.9 %collective-permute-start.12 = (bf16[2,512,128]{2,1,0:T(8,128)(2,1)S(1)}, bf16[2,512,128]{2,1,0:T(8,128)(2,1)S(1)}, u32[]{:S(2)}, u32[]{:S(2)}) collective-permute-start(bf16[2,512,128]{2,1,0:T(8,128)(2,1)S(1)} %get-tuple-element.69), channel_id=1, source_target_pairs={{3,0},{2,1},{5,2},{4,3},{7,4},{6,5},{9,6},{8,7},{11,8},{10,9},{13,... | collective-permute-start | bytes 786440 | tf_op jit(solution)/shard_map/ppermute | solution.py:399
  53.0 1.9 %collective-permute-start.13 = (bf16[2,512,128]{2,1,0:T(8,128)(2,1)S(1)}, bf16[2,512,128]{2,1,0:T(8,128)(2,1)S(1)}, u32[]{:S(2)}, u32[]{:S(2)}) collective-permute-start(bf16[2,512,128]{2,1,0:T(8,128)(2,1)S(1)} %get-tuple-element.73), channel_id=1, source_target_pairs={{2,0},{3,1},{4,2},{5,3},{6,4},{7,5},{8,6},{9,7},{10,8},{11,9},{12,... | collective-permute-start | bytes 786440 | tf_op jit(solution)/shard_map/ppermute | solution.py:399
  54.9 0.6 collective-permute-start.14
  55.5 1.1 %early_grads.1 = (bf16[512,512]{1,0:T(8,128)(2,1)}, bf16[512,512]{1,0:T(8,128)(2,1)}) custom-call(s32[1]{0:T(128)} %bitcast.core, bf16[2,512,128]{2,1,0:T(8,128)(2,1)S(1)} %get-tuple-element.65.refs_0_, bf16[2,512,128]{2,1,0:T(8,128)(2,1)S(1)} %collective-permute-done.11.refs_1_), custom_call_target="tpu_custom_call" | custom-call | tf_op jit(solution)/shard_map/early_grads/pallas_call | solution.py:331
  56.6 2.1 %place.1 = (bf16[512,2048]{1,0:T(8,128)(2,1)}, bf16[512,2048]{1,0:T(8,128)(2,1)}) custom-call(s32[1]{0:T(128)} %bitcast.core, bf16[2,512,512]{2,1,0:T(8,128)(2,1)S(1)} %collective-permute-done.6.refs_0_, bf16[2,512,512]{2,1,0:T(8,128)(2,1)S(1)} %collective-permute-done.10.refs_1_, ...), custom_call_target="tpu_custom_call", output_to_operand_aliasing={{0}: (3, {}), {1}: (4, {})} | custom-call | tf_op jit(solution)/shard_map/place/pallas_call | solution.py:285
  58.7 3.8 %collective-permute-done.12.other_back = bf16[2,512,128]{2,1,0:T(8,128)(2,1)S(1)} collective-permute-done((bf16[2,512,128]{2,1,0:T(8,128)(2,1)S(1)}, bf16[2,512,128]{2,1,0:T(8,128)(2,1)S(1)}, u32[]{:S(2)}, u32[]{:S(2)}) %collective-permute-start.12) | collective-permute-done | bytes 262176 | tf_op jit(solution)/shard_map/ppermute | solution.py:399
  62.5 5.5 %collective-permute-done.13.own_back = bf16[2,512,128]{2,1,0:T(8,128)(2,1)S(1)} collective-permute-done((bf16[2,512,128]{2,1,0:T(8,128)(2,1)S(1)}, bf16[2,512,128]{2,1,0:T(8,128)(2,1)S(1)}, u32[]{:S(2)}, u32[]{:S(2)}) %collective-permute-start.13) | collective-permute-done | bytes 262176 | tf_op jit(solution)/shard_map/ppermute | solution.py:399
  68.0 0.9 %last_grads.1 = (bf16[512,512]{1,0:T(8,128)(2,1)}, bf16[512,512]{1,0:T(8,128)(2,1)}) custom-call(s32[1]{0:T(128)} %bitcast.core, f32[2,512,128]{2,1,0:T(8,128)S(1)} %get-tuple-element.72.own_part, bf16[2,512,128]{2,1,0:T(8,128)(2,1)S(1)} %collective-permute-done.13.own_back, ...), custom_call_target="tpu_custom_call", output_to_operand_aliasing={{0}: (5, {}), {1}: (6, {})} | custom-call | tf_op jit(solution)/shard_map/last_grads/pallas_call | solution.py:370
  (10 shorter events, 0.1 us)
Async XLA Ops:
  0.6 18.9 %copy-start = (s32[8]{0:T(128)S(1)}, s32[8]{0:T(128)}, u32[]{:S(2)}) copy-start(s32[8]{0:T(128)} %refs_1_.3) | copy-start | bytes 100
  2.0 17.5 %collective-permute-start.1 = (bf16[512,2048]{1,0:T(8,128)(2,1)}, bf16[512,2048]{1,0:T(8,128)(2,1)S(1)}, u32[]{:S(2)}, u32[]{:S(2)}) collective-permute-start(bf16[512,2048]{1,0:T(8,128)(2,1)} %refs_3_.3), channel_id=1, source_target_pairs={{0,1},{1,0},{2,3},{3,2},{4,5},{5,4},{6,7},{7,6},{8,9},{9,8},{10,11... | collective-permute-start | bytes 6291464 | tf_op jit(solution)/shard_map/ppermute | solution.py:399
  2.8 16.8 %collective-permute-start.2 = (bf16[512,2048]{1,0:T(8,128)(2,1)}, bf16[512,2048]{1,0:T(8,128)(2,1)}, u32[]{:S(2)}, u32[]{:S(2)}) collective-permute-start(bf16[512,2048]{1,0:T(8,128)(2,1)} %refs_4_.3), channel_id=1, source_target_pairs={{0,1},{1,0},{2,3},{3,2},{4,5},{5,4},{6,7},{7,6},{8,9},{9,8},{10,11... | collective-permute-start | bytes 6291464 | tf_op jit(solution)/shard_map/ppermute | solution.py:399
  2.9 9.5 %collective-permute-start.7 = (bf16[2,512,128]{2,1,0:T(8,128)(2,1)S(1)}, bf16[2,512,128]{2,1,0:T(8,128)(2,1)S(1)}, u32[]{:S(2)}, u32[]{:S(2)}) collective-permute-start(bf16[2,512,128]{2,1,0:T(8,128)(2,1)S(1)} %get-tuple-element.45), channel_id=1, source_target_pairs={{0,1},{1,0},{2,3},{3,2},{4,5},{5,4},{6,7},{7,6},{8,9},{9,8},{10,11... | collective-permute-start | bytes 786440 | tf_op jit(solution)/shard_map/ppermute | solution.py:399
  3.3 5.7 %collective-permute-start = (s32[4,6]{1,0:T(4,128)}, s32[4,6]{1,0:T(4,128)S(1)}, u32[]{:S(2)}, u32[]{:S(2)}) collective-permute-start(s32[4,6]{1,0:T(4,128)} %param.11), channel_id=1, source_target_pairs={{0,1},{1,0},{2,3},{3,2},{4,5},{5,4},{6,7},{7,6},{8,9},{9,8},{10,11... | collective-permute-start | bytes 296 | tf_op jit(solution)/shard_map/ppermute | solution.py:399
  3.4 10.0 %collective-permute-start.4 = (bf16[2,512,128]{2,1,0:T(8,128)(2,1)S(1)}, bf16[2,512,128]{2,1,0:T(8,128)(2,1)S(1)}, u32[]{:S(2)}, u32[]{:S(2)}) collective-permute-start(bf16[2,512,128]{2,1,0:T(8,128)(2,1)S(1)} %get-tuple-element.42.refs_7_), channel_id=1, source_target_pairs={{0,2},{1,3},{2,4},{3,5},{4,6},{5,7},{6,8},{7,9},{8,10},{9,11},{10,... | collective-permute-start | bytes 786440 | tf_op jit(solution)/shard_map/ppermute | solution.py:399
  9.0 10.6 %collective-permute-start.5 = (bf16[2,512,128]{2,1,0:T(8,128)(2,1)S(1)}, bf16[2,512,128]{2,1,0:T(8,128)(2,1)}, u32[]{:S(2)}, u32[]{:S(2)}) collective-permute-start(bf16[2,512,128]{2,1,0:T(8,128)(2,1)S(1)} %get-tuple-element.43), channel_id=1, source_target_pairs={{0,3},{1,2},{2,5},{3,4},{4,7},{5,6},{6,9},{7,8},{8,11},{9,10},{10,... | collective-permute-start | bytes 786440 | tf_op jit(solution)/shard_map/ppermute | solution.py:399
  12.4 7.2 %collective-permute-start.3 = (bf16[2,512,128]{2,1,0:T(8,128)(2,1)S(1)}, bf16[2,512,128]{2,1,0:T(8,128)(2,1)}, u32[]{:S(2)}, u32[]{:S(2)}) collective-permute-start(bf16[2,512,128]{2,1,0:T(8,128)(2,1)S(1)} %get-tuple-element.43), channel_id=1, source_target_pairs={{0,1},{1,0},{2,3},{3,2},{4,5},{5,4},{6,7},{7,6},{8,9},{9,8},{10,11... | collective-permute-start | bytes 786440 | tf_op jit(solution)/shard_map/ppermute | solution.py:399
  13.4 22.6 %collective-permute-start.8 = (bf16[2,1024,128]{2,1,0:T(8,128)(2,1)S(1)}, bf16[2,1024,128]{2,1,0:T(8,128)(2,1)S(1)}, u32[]{:S(2)}, u32[]{:S(2)}) collective-permute-start(bf16[2,1024,128]{2,1,0:T(8,128)(2,1)S(1)} %pad_maximum_fusion), channel_id=1, source_target_pairs={{0,2},{1,3},{2,4},{3,5},{4,6},{5,7},{6,8},{7,9},{8,10},{9,11},{10,... | collective-permute-start | bytes 1572872 | tf_op jit(solution)/shard_map/ppermute | solution.py:399
  33.8 16.3 %collective-permute-start.9 = (bf16[2,1024,128]{2,1,0:T(8,128)(2,1)S(1)}, bf16[2,1024,128]{2,1,0:T(8,128)(2,1)S(1)}, u32[]{:S(2)}, u32[]{:S(2)}) collective-permute-start(bf16[2,1024,128]{2,1,0:T(8,128)(2,1)S(1)} %get-tuple-element.57), channel_id=1, source_target_pairs={{2,0},{3,1},{4,2},{5,3},{6,4},{7,5},{8,6},{9,7},{10,8},{11,9},{12,... | collective-permute-start | bytes 1572872 | tf_op jit(solution)/shard_map/ppermute | solution.py:399
  35.9 20.7 %collective-permute-start.6 = (bf16[2,512,512]{2,1,0:T(8,128)(2,1)S(1)}, bf16[2,512,512]{2,1,0:T(8,128)(2,1)S(1)}, u32[]{:S(2)}, u32[]{:S(2)}) collective-permute-start(bf16[2,512,512]{2,1,0:T(8,128)(2,1)S(1)} %get-tuple-element.49), channel_id=1, source_target_pairs={{0,1},{1,0},{2,3},{3,2},{4,5},{5,4},{6,7},{7,6},{8,9},{9,8},{10,11... | collective-permute-start | bytes 3145736 | tf_op jit(solution)/shard_map/ppermute | solution.py:399
  50.1 6.5 %collective-permute-start.10 = (bf16[2,512,512]{2,1,0:T(8,128)(2,1)S(1)}, bf16[2,512,512]{2,1,0:T(8,128)(2,1)S(1)}, u32[]{:S(2)}, u32[]{:S(2)}) collective-permute-start(bf16[2,512,512]{2,1,0:T(8,128)(2,1)S(1)} %get-tuple-element.58), channel_id=1, source_target_pairs={{0,1},{1,0},{2,3},{3,2},{4,5},{5,4},{6,7},{7,6},{8,9},{9,8},{10,11... | collective-permute-start | bytes 3145736 | tf_op jit(solution)/shard_map/ppermute | solution.py:399
  51.0 3.9 %collective-permute-start.11 = (bf16[2,512,128]{2,1,0:T(8,128)(2,1)S(1)}, bf16[2,512,128]{2,1,0:T(8,128)(2,1)S(1)}, u32[]{:S(2)}, u32[]{:S(2)}) collective-permute-start(bf16[2,512,128]{2,1,0:T(8,128)(2,1)S(1)} %get-tuple-element.66), channel_id=1, source_target_pairs={{0,1},{1,0},{2,3},{3,2},{4,5},{5,4},{6,7},{7,6},{8,9},{9,8},{10,11... | collective-permute-start | bytes 786440 | tf_op jit(solution)/shard_map/ppermute | solution.py:399
  51.1 11.4 %collective-permute-start.12 = (bf16[2,512,128]{2,1,0:T(8,128)(2,1)S(1)}, bf16[2,512,128]{2,1,0:T(8,128)(2,1)S(1)}, u32[]{:S(2)}, u32[]{:S(2)}) collective-permute-start(bf16[2,512,128]{2,1,0:T(8,128)(2,1)S(1)} %get-tuple-element.69), channel_id=1, source_target_pairs={{3,0},{2,1},{5,2},{4,3},{7,4},{6,5},{9,6},{8,7},{11,8},{10,9},{13,... | collective-permute-start | bytes 786440 | tf_op jit(solution)/shard_map/ppermute | solution.py:399
  53.0 15.0 %collective-permute-start.13 = (bf16[2,512,128]{2,1,0:T(8,128)(2,1)S(1)}, bf16[2,512,128]{2,1,0:T(8,128)(2,1)S(1)}, u32[]{:S(2)}, u32[]{:S(2)}) collective-permute-start(bf16[2,512,128]{2,1,0:T(8,128)(2,1)S(1)} %get-tuple-element.73), channel_id=1, source_target_pairs={{2,0},{3,1},{4,2},{5,3},{6,4},{7,5},{8,6},{9,7},{10,8},{11,9},{12,... | collective-permute-start | bytes 786440 | tf_op jit(solution)/shard_map/ppermute | solution.py:399
  54.9 13.0 %collective-permute-start.14 = (bf16[2,512,128]{2,1,0:T(8,128)(2,1)S(1)}, bf16[2,512,128]{2,1,0:T(8,128)(2,1)S(1)}, u32[]{:S(2)}, u32[]{:S(2)}) collective-permute-start(bf16[2,512,128]{2,1,0:T(8,128)(2,1)S(1)} %get-tuple-element.74), channel_id=1, source_target_pairs={{0,1},{1,0},{2,3},{3,2},{4,5},{5,4},{6,7},{7,6},{8,9},{9,8},{10,11... | collective-permute-start | bytes 786440 | tf_op jit(solution)/shard_map/ppermute | solution.py:399
